TPU v7x, 32 devices: a whole 2x2x4 slice. The times are simulated.
32 devices in a mesh: rep: 4 (over z), shard: 4 (over y, x), seq: 2 (over core).
Axes of the slice: x: 2, y: 2, z: 4, core: 2. Of those that a mesh axis runs over, the one named last changes fastest.
Arguments:
- tokens_in: bfloat16 [4096, 1024], P(('rep', 'shard', 'seq')), may hold values from -6 to 6
- doc_lengths: int32 [4, 4], P('rep'), may hold values from 1 to 512, 1024 in all within a row
- attn_gain: float32 [1024], replicated, may hold values from 0.25 to 1.75
- w_query: bfloat16 [1024, 1024], P('shard'), may hold values from -0.1875 to 0.1875
- key_weight: bfloat16 [1024, 512], P('shard'), may hold values from -0.1875 to 0.1875
- value_weight: bfloat16 [1024, 512], P('shard'), may hold values from -0.1875 to 0.1875
- w_output: bfloat16 [1024, 1024], P('shard'), may hold values from -2 to 2
- query_norm_gain: float32 [64], replicated, may hold values from 0.5 to 2
- key_norm_gain: float32 [64], replicated, may hold values from 0.5 to 2
- mlp_gain: float32 [1024], replicated, may hold values from 0.25 to 1.75
- w_gate: bfloat16 [4608, 1024], P('shard'), may hold values from -0.1875 to 0.1875
- w_up: bfloat16 [4608, 1024], P('shard'), may hold values from -0.1875 to 0.1875
- w_down: bfloat16 [4608, 1024], P('shard'), may hold values from -0.09375 to 0.09375
- out_grad: bfloat16 [4096, 1024], P(('rep', 'shard', 'seq')), may hold values from -6 to 6
Outputs:
- act_out: float32 [4096, 1024], P(('rep', 'shard', 'seq'))
- in_grad: float32 [4096, 1024], P(('rep', 'shard', 'seq'))
- grad_attn_gain: float32 [1024], replicated
- grad_query: float32 [1024, 1024], P(('shard', 'seq'))
- grad_key: float32 [1024, 512], P(('shard', 'seq'))
- grad_value: float32 [1024, 512], P(('shard', 'seq'))
- grad_output: float32 [1024, 1024], P(('shard', 'seq'))
- grad_query_gain: float32 [64], replicated
- grad_key_gain: float32 [64], replicated
- grad_mlp_gain: float32 [1024], replicated
- grad_gate: float32 [4608, 1024], P(('shard', 'seq'))
- grad_up: float32 [4608, 1024], P(('shard', 'seq'))
- grad_down: float32 [4608, 1024], P(('shard', 'seq'))
Inputs may be any that keep to these rules, and one draw needn't show every extreme that they name: `doc_lengths`: each row sums to 1024, and its largest entry is exactly 512.
All inputs are finite; a program needn't handle non-finite values.
Results may differ from a plain program's by a relative error of at most 0.014.
The roundings to bfloat16 on the way count: a program that leaves them out, or rounds other values in their place, can miss the bound.
Values may be sent and summed in bfloat16 or wider, within the bound.
No kernel may reach another device: no remote copies, remote signals or barrier semaphores. Data moves between devices by JAX's collectives and lax.ppermute only.
A program may use at most 256 MiB of HBM per device.

v0:
```python
import math

import jax
import jax.numpy as jnp
from jax import lax
from jax.experimental import pallas as pl
from jax.experimental.pallas import tpu as pltpu
from jax.sharding import PartitionSpec as P

norm_eps = 1e-05
rope_base = 1000000.0
very_low = -1e30
contract_last = (((1,), (1,)), ((), ()))
contract_first = (((0,), (0,)), ((), ()))


def rms_scale(values):
    return lax.rsqrt(jnp.mean(values * values, axis=-1, keepdims=True) + norm_eps)


def root_mean_backward(normed, factor, gain, upstream):
    scaled = upstream * gain
    return factor * (scaled - normed * jnp.mean(scaled * normed, axis=-1, keepdims=True))


def rope_tables(positions, head_dim):
    half_dim = head_dim // 2
    inverse_freq = rope_base ** (-(jnp.arange(half_dim, dtype=jnp.float32) * 2.0 / head_dim))
    angles = positions.astype(jnp.float32)[:, None] * inverse_freq[None, :]
    return (jnp.cos(angles)[:, None, :], jnp.sin(angles)[:, None, :])


def rotate_pairs(values, cosine_table, sine_values):
    half_dim = values.shape[-1] // 2
    lower_half = values[..., :half_dim]
    upper_half = values[..., half_dim:]
    return jnp.concatenate(
        [
            lower_half * cosine_table - upper_half * sine_values,
            upper_half * cosine_table + lower_half * sine_values,
        ],
        axis=-1,
    )


def rotate_back(grads, cosine_table, sine_values):
    half_dim = grads.shape[-1] // 2
    lower_half = grads[..., :half_dim]
    upper_half = grads[..., half_dim:]
    return jnp.concatenate(
        [
            lower_half * cosine_table + upper_half * sine_values,
            upper_half * cosine_table - lower_half * sine_values,
        ],
        axis=-1,
    )


def doc_info(lengths, positions):
    doc_ends = jnp.cumsum(lengths)
    finished = doc_ends[None, :] <= positions[:, None]
    doc_ids = jnp.sum(finished.astype(jnp.int32), axis=1)
    doc_first = jnp.sum(jnp.where(finished, lengths[None, :], 0), axis=1)
    return (doc_ids, positions - doc_first)


def local(
    tokens_in,
    doc_lengths,
    attn_gain,
    w_query,
    key_weight,
    value_weight,
    w_output,
    query_norm_gain,
    key_norm_gain,
    mlp_gain,
    w_gate,
    w_up,
    w_down,
    out_grad,
):
    row_count = tokens_in.shape[0]
    model_width = tokens_in.shape[1]
    head_dim = query_norm_gain.shape[0]
    query_width = w_query.shape[1]
    kv_width = key_weight.shape[1]
    kv_heads = kv_width // head_dim
    head_grouping = query_width // kv_width
    score_scale = head_dim ** (-0.5)
    rank_count = lax.axis_size("shard") * lax.axis_size("seq")
    group_rows = row_count * rank_count
    first_row = lax.axis_index(("shard", "seq")) * row_count
    key_block = min(512, group_rows)
    block_count = group_rows // key_block
    key_index = jnp.arange(group_rows, dtype=jnp.int32)
    key_docs, key_offset = doc_info(doc_lengths[0], key_index)
    query_index = first_row + jnp.arange(row_count, dtype=jnp.int32)
    query_docs = lax.dynamic_slice_in_dim(key_docs, first_row, row_count)
    query_offset = lax.dynamic_slice_in_dim(key_offset, first_row, row_count)
    cosine_table, sine_values = rope_tables(query_offset, head_dim)
    x_float = tokens_in.astype(jnp.float32)
    norm_one = rms_scale(x_float)
    x_hat = x_float * norm_one
    normalized_input = (x_hat * attn_gain).astype(jnp.bfloat16)
    pieces = (
        lax.all_gather(w_query, "shard", axis=0, tiled=True),
        lax.all_gather(key_weight, "shard", axis=0, tiled=True),
        lax.all_gather(value_weight, "shard", axis=0, tiled=True),
    )
    in_cols = normalized_input
    queries, key_proj, value_proj = tuple(
        (jnp.dot(in_cols, weight, preferred_element_type=jnp.float32) for weight in pieces)
    )
    query_heads = queries.reshape(row_count, query_width // head_dim, head_dim)
    query_norm = rms_scale(query_heads)
    query_normalized = query_heads * query_norm
    query_rotated = rotate_pairs(
        query_normalized * query_norm_gain, cosine_table, sine_values
    ).astype(jnp.bfloat16)
    key_head_rows = key_proj.reshape(row_count, kv_heads, head_dim)
    key_head_norm = rms_scale(key_head_rows)
    key_normalized = key_head_rows * key_head_norm
    key_rot = rotate_pairs(key_normalized * key_norm_gain, cosine_table, sine_values).astype(
        jnp.bfloat16
    )
    value_rows = value_proj.astype(jnp.bfloat16)
    key_all, value_all = (
        lax.all_gather(key_rot.reshape(row_count, kv_width), ("shard", "seq"), axis=0, tiled=True),
        lax.all_gather(value_rows, ("shard", "seq"), axis=0, tiled=True),
    )
    query_grouped = query_rotated.reshape(row_count, kv_heads, head_grouping, head_dim)

    def block_mask(offset, span_rows):
        docs_here = lax.dynamic_slice_in_dim(key_docs, offset, span_rows)
        index_here = offset + jnp.arange(span_rows, dtype=jnp.int32)
        return (query_docs[:, None] == docs_here[None, :]) & (
            index_here[None, :] <= query_index[:, None]
        )

    def block_scores(offset, span_rows, allowed):
        key_rows = lax.dynamic_slice_in_dim(key_all, offset, span_rows, 0).reshape(
            span_rows, kv_heads, head_dim
        )
        value_block = lax.dynamic_slice_in_dim(value_all, offset, span_rows, 0).reshape(
            span_rows, kv_heads, head_dim
        )
        scores = (
            jnp.einsum(
                "tgjd,rgd->gjtr", query_grouped, key_rows, preferred_element_type=jnp.float32
            )
            * score_scale
        )
        return (jnp.where(allowed, scores, very_low), key_rows, value_block)

    def total_block(block_index, running):
        offset = block_index * key_block
        allowed = block_mask(offset, key_block)

        def total_accumulate(softmax_state):
            row_high, row_total = softmax_state
            scores, _, _ = block_scores(offset, key_block, allowed)
            new_high = jnp.maximum(row_high, jnp.max(scores, axis=-1))
            exp_scores = jnp.where(allowed, jnp.exp(scores - new_high[..., None]), 0.0)
            row_total = row_total * jnp.exp(row_high - new_high) + jnp.sum(exp_scores, axis=-1)
            return (new_high, row_total)

        return lax.cond(
            jnp.any(allowed), total_accumulate, lambda softmax_state: softmax_state, running
        )

    softmax_init = (
        jnp.full((kv_heads, head_grouping, row_count), very_low, jnp.float32),
        jnp.zeros((kv_heads, head_grouping, row_count), jnp.float32),
    )
    row_high, row_total = lax.fori_loop(0, block_count, total_block, softmax_init)
    log_total = row_high + jnp.log(row_total)

    def mix_block(block_index, weighted):
        offset = block_index * key_block
        allowed = block_mask(offset, key_block)

        def mix_accumulate(current):
            scores, _, value_block = block_scores(offset, key_block, allowed)
            attn_prob = jnp.where(allowed, jnp.exp(scores - log_total[..., None]), 0.0).astype(
                jnp.bfloat16
            )
            return current + jnp.einsum(
                "gjtr,rgd->gjtd", attn_prob, value_block, preferred_element_type=jnp.float32
            )

        return lax.cond(jnp.any(allowed), mix_accumulate, lambda current: current, weighted)

    weighted = lax.fori_loop(
        0,
        block_count,
        mix_block,
        jnp.zeros((kv_heads, head_grouping, row_count, head_dim), jnp.float32),
    )
    head_mixture = (
        weighted.transpose(2, 0, 1, 3).reshape(row_count, query_width).astype(jnp.bfloat16)
    )
    attn_part = lax.dot_general(
        head_mixture,
        lax.all_gather(w_output, "shard", axis=0, tiled=True),
        contract_last,
        preferred_element_type=jnp.float32,
    )
    residual = x_float + attn_part
    norm_two = rms_scale(residual)
    resid_hat = residual * norm_two
    normed_mid = (resid_hat * mlp_gain).astype(jnp.bfloat16)
    gate_rows = lax.all_gather(w_gate, "shard", axis=0, tiled=True)
    up_rows = lax.all_gather(w_up, "shard", axis=0, tiled=True)
    down_rows = lax.all_gather(w_down, "shard", axis=0, tiled=True)
    gate_part = lax.dot_general(
        normed_mid, gate_rows, contract_last, preferred_element_type=jnp.float32
    )
    up_part = lax.dot_general(
        normed_mid, up_rows, contract_last, preferred_element_type=jnp.float32
    )
    hidden_part = (gate_part * jax.nn.sigmoid(gate_part) * up_part).astype(jnp.bfloat16)
    mlp_sum = jnp.dot(hidden_part, down_rows, preferred_element_type=jnp.float32)
    mlp_gate_store = gate_part
    mlp_up_store = up_part
    hidden_store = hidden_part
    mlp_sum, gate_store, up_store, hidden_store = (
        mlp_sum,
        mlp_gate_store,
        mlp_up_store,
        hidden_store,
    )
    act_out = residual + mlp_sum
    grad_float = out_grad.astype(jnp.float32)
    gate_rows = lax.all_gather(w_gate, "shard", axis=0, tiled=True)
    up_rows = lax.all_gather(w_up, "shard", axis=0, tiled=True)
    down_rows = lax.all_gather(w_down, "shard", axis=0, tiled=True)
    gate_part = gate_store
    up_part = up_store
    grad_hidden = lax.dot_general(
        out_grad, down_rows, contract_last, preferred_element_type=jnp.float32
    )
    gate_sig = jax.nn.sigmoid(gate_part)
    gate_grad = (grad_hidden * up_part * gate_sig * (1.0 + gate_part * (1.0 - gate_sig))).astype(
        jnp.bfloat16
    )
    up_grad = (grad_hidden * gate_part * gate_sig).astype(jnp.bfloat16)
    grad_mid = jnp.dot(gate_grad, gate_rows, preferred_element_type=jnp.float32) + jnp.dot(
        up_grad, up_rows, preferred_element_type=jnp.float32
    )
    gate_grad_store = gate_grad
    up_grad_store = up_grad
    grad_mid, gate_grad_store, up_grad_store = (grad_mid, gate_grad_store, up_grad_store)
    grad_resid = grad_float + root_mean_backward(resid_hat, norm_two, mlp_gain, grad_mid)
    mlp_gain_part = jnp.sum(grad_mid * resid_hat, axis=0)
    grad_resid_b = grad_resid.astype(jnp.bfloat16)
    resid_cols = grad_resid_b
    mixing_gradient = jnp.dot(
        resid_cols,
        lax.all_gather(w_output, "shard", axis=0, tiled=True),
        preferred_element_type=jnp.float32,
    ).astype(jnp.bfloat16)
    mix_grouped = mixing_gradient.reshape(row_count, kv_heads, head_grouping, head_dim)
    delta_row_values = jnp.sum(
        (mixing_gradient.astype(jnp.float32) * head_mixture.astype(jnp.float32)).reshape(
            row_count, kv_heads, head_grouping, head_dim
        ),
        axis=-1,
    ).transpose(1, 2, 0)

    def score_grads(offset, span_rows, allowed):
        scores, key_rows, value_block = block_scores(offset, span_rows, allowed)
        attn_prob = jnp.where(allowed, jnp.exp(scores - log_total[..., None]), 0.0)
        grad_prob = jnp.einsum(
            "tgjd,rgd->gjtr", mix_grouped, value_block, preferred_element_type=jnp.float32
        )
        grad_score = (attn_prob * (grad_prob - delta_row_values[..., None])).astype(jnp.bfloat16)
        return (attn_prob, grad_score, key_rows)

    def query_pass(block_index, grad_sum):
        offset = block_index * key_block
        allowed = block_mask(offset, key_block)

        def query_accumulate(current):
            _, grad_score, key_rows = score_grads(offset, key_block, allowed)
            return current + score_scale * jnp.einsum(
                "gjtr,rgd->tgjd", grad_score, key_rows, preferred_element_type=jnp.float32
            )

        return lax.cond(jnp.any(allowed), query_accumulate, lambda current: current, grad_sum)

    query_rot_grad = lax.fori_loop(
        0,
        block_count,
        query_pass,
        jnp.zeros((row_count, kv_heads, head_grouping, head_dim), jnp.float32),
    )

    def one_block(start_row):
        allowed = block_mask(start_row, key_block)

        def compute(unused):
            attn_prob, grad_score, _ = score_grads(start_row, key_block, allowed)
            key_grad = score_scale * jnp.einsum(
                "gjtr,tgjd->rgd", grad_score, query_grouped, preferred_element_type=jnp.float32
            )
            value_grad = jnp.einsum(
                "gjtr,tgjd->rgd",
                attn_prob.astype(jnp.bfloat16),
                mix_grouped,
                preferred_element_type=jnp.float32,
            )
            return jnp.concatenate(
                [key_grad.reshape(key_block, kv_width), value_grad.reshape(key_block, kv_width)],
                axis=1,
            )

        return lax.cond(
            jnp.any(allowed),
            compute,
            lambda unused: jnp.zeros((key_block, 2 * kv_width), jnp.float32),
            0,
        )

    starts = key_block * jnp.arange(
        row_count * lax.axis_size(("shard", "seq")) // key_block, dtype=jnp.int32
    )
    kv_summed = lax.psum_scatter(
        lax.map(one_block, starts).reshape(
            row_count * lax.axis_size(("shard", "seq")), 2 * kv_width
        ),
        ("shard", "seq"),
        scatter_dimension=0,
        tiled=True,
    )
    key_rot_grad = kv_summed[:, :kv_width].reshape(row_count, kv_heads, head_dim)
    value_grad_b = kv_summed[:, kv_width:].astype(jnp.bfloat16)
    key_unrotated = rotate_back(key_rot_grad, cosine_table, sine_values)
    key_gain_part = jnp.sum(key_unrotated * key_normalized, axis=(0, 1))
    key_row_gradient = (
        root_mean_backward(key_normalized, key_head_norm, key_norm_gain, key_unrotated)
        .reshape(row_count, kv_width)
        .astype(jnp.bfloat16)
    )
    query_unrot = rotate_back(
        query_rot_grad.reshape(row_count, query_width // head_dim, head_dim),
        cosine_table,
        sine_values,
    )
    query_gain_part = jnp.sum(query_unrot * query_normalized, axis=(0, 1))
    grad_query_rows = (
        root_mean_backward(query_normalized, query_norm, query_norm_gain, query_unrot)
        .reshape(row_count, query_width)
        .astype(jnp.bfloat16)
    )
    query_rows, key_rows, value_rows_w = lax.all_gather(
        (w_query, key_weight, value_weight), "shard", axis=0, tiled=True
    )
    grad_in_norm = (
        lax.dot_general(
            grad_query_rows, query_rows, contract_last, preferred_element_type=jnp.float32
        )
        + lax.dot_general(
            key_row_gradient, key_rows, contract_last, preferred_element_type=jnp.float32
        )
        + lax.dot_general(
            value_grad_b, value_rows_w, contract_last, preferred_element_type=jnp.float32
        )
    )
    in_grad = grad_resid + root_mean_backward(x_hat, norm_one, attn_gain, grad_in_norm)
    attn_gain_part = jnp.sum(grad_in_norm * x_hat, axis=0)
    grad_attn_gain, grad_mlp_gain, grad_query_gain, grad_key_gain = lax.psum(
        (attn_gain_part, mlp_gain_part, query_gain_part, key_gain_part), ("rep", "shard", "seq")
    )
    attn_grads = jnp.concatenate([grad_query_rows, key_row_gradient, value_grad_b], axis=1)
    d_share = model_width // rank_count
    in_own, resid_own, gate_own, up_own, hidden_own = (
        lax.all_to_all(normalized_input, ("shard", "seq"), split_axis=1, concat_axis=0, tiled=True),
        lax.all_to_all(grad_resid_b, ("shard", "seq"), split_axis=1, concat_axis=0, tiled=True),
        lax.all_to_all(gate_grad_store, ("shard", "seq"), split_axis=1, concat_axis=0, tiled=True),
        lax.all_to_all(up_grad_store, ("shard", "seq"), split_axis=1, concat_axis=0, tiled=True),
        lax.all_to_all(hidden_store, ("shard", "seq"), split_axis=1, concat_axis=0, tiled=True),
    )
    attn_piece = lax.all_gather(attn_grads, ("shard", "seq"), axis=0, tiled=True)
    mix_piece = lax.all_gather(head_mixture, ("shard", "seq"), axis=0, tiled=True)
    mid_piece = lax.all_gather(normed_mid, ("shard", "seq"), axis=0, tiled=True)
    grad_piece = lax.all_gather(out_grad, ("shard", "seq"), axis=0, tiled=True)
    in_cols = in_own
    resid_cols = resid_own
    attn_rows = jnp.concatenate(
        [
            lax.dot_general(
                in_cols, attn_piece, contract_first, preferred_element_type=jnp.float32
            ),
            lax.dot_general(
                resid_cols, mix_piece, contract_first, preferred_element_type=jnp.float32
            ),
        ],
        axis=1,
    )
    mlp_rows = jnp.concatenate(
        [
            lax.dot_general(
                gate_own, mid_piece, contract_first, preferred_element_type=jnp.float32
            ),
            lax.dot_general(up_own, mid_piece, contract_first, preferred_element_type=jnp.float32),
            lax.dot_general(
                hidden_own, grad_piece, contract_first, preferred_element_type=jnp.float32
            ),
        ],
        axis=1,
    )
    group_grads = jnp.concatenate([attn_rows, mlp_rows], axis=0)
    own_grads = lax.psum(group_grads, "rep")
    attn_block_grads = own_grads[:d_share]
    mlp_block_grads = own_grads[d_share:]
    grad_query = attn_block_grads[:, :query_width]
    grad_key = attn_block_grads[:, query_width : query_width + kv_width]
    grad_value = attn_block_grads[:, query_width + kv_width : query_width + 2 * kv_width]
    grad_output = attn_block_grads[:, query_width + 2 * kv_width :]
    grad_gate = mlp_block_grads[:, :model_width]
    grad_up = mlp_block_grads[:, model_width : 2 * model_width]
    grad_down = mlp_block_grads[:, 2 * model_width :]
    return (
        act_out,
        in_grad,
        grad_attn_gain,
        grad_query,
        grad_key,
        grad_value,
        grad_output,
        grad_query_gain,
        grad_key_gain,
        grad_mlp_gain,
        grad_gate,
        grad_up,
        grad_down,
    )


group_axes = ("shard", "seq")


def group_swap(values, mask):
    return lax.ppermute(values, group_axes, [(rank, rank ^ mask) for rank in range(8)])


def rep_swap(values, mask):
    return lax.ppermute(values, "rep", [(rank, rank ^ mask) for rank in range(4)])


xor_order = (0, 2, 4, 6, 1, 3, 5, 7)


def gather_near(own):
    return [own] + [group_swap(own, mask) for mask in (2, 4, 6)]


def gather_far(near):
    return [group_swap(piece, 1) for piece in near]


def after(values, marker):
    return lax.optimization_barrier((values, marker))[0]


def add_rounded(left, right):
    return (left.astype(jnp.float32) + right.astype(jnp.float32)).astype(jnp.bfloat16)


def scatter_sum(near_part, far_part):
    swapped = group_swap(far_part.astype(jnp.bfloat16), 1)
    width = near_part.shape[0] // 4
    halves = [
        near_part[at : at + width] + swapped[at : at + width].astype(jnp.float32)
        for at in range(0, 4 * width, width)
    ]
    total = halves[0]
    moved = [
        group_swap(half.astype(jnp.bfloat16), mask) for mask, half in zip((2, 4, 6), halves[1:])
    ]
    for piece in moved:
        total = total + piece.astype(jnp.float32)
    return total


def rep_halving_sum(values, first_marker, second_marker):
    place = lax.axis_index("rep")
    low = place % 2
    high = place // 2
    half = values.shape[0] // 2
    quarter = half // 2
    kept = lax.dynamic_slice_in_dim(values, low * half, half)
    sent = lax.dynamic_slice_in_dim(values, (1 - low) * half, half)
    part = add_rounded(*after((kept, rep_swap(sent, 1)), first_marker))
    kept = lax.dynamic_slice_in_dim(part, high * quarter, quarter)
    sent = lax.dynamic_slice_in_dim(part, (1 - high) * quarter, quarter)
    part = add_rounded(*after((kept, rep_swap(sent, 2)), second_marker))
    other = rep_swap(part, 2)
    part = jnp.where(
        high == 0, jnp.concatenate([part, other]), jnp.concatenate([other, part])
    )
    other = rep_swap(part, 1)
    return jnp.where(low == 0, jnp.concatenate([part, other]), jnp.concatenate([other, part]))


def sum_everywhere(values):
    for mask in (1, 2, 4):
        values = values + group_swap(values, mask)
    for mask in (1, 2):
        values = values + rep_swap(values, mask)
    return values


def lower_lanes(shape, width):
    return lax.broadcasted_iota(jnp.int32, shape, 1) % (2 * width) < width


def pair_scale(values, head_dim):
    lower = lower_lanes(values.shape, head_dim)
    low = jnp.sum(jnp.where(lower, values, 0.0), axis=1, keepdims=True)
    high = jnp.sum(jnp.where(lower, 0.0, values), axis=1, keepdims=True)
    return jnp.where(lower, low, high) * (1.0 / head_dim)


def swap_halves(values, head_dim):
    width = values.shape[1]
    half = head_dim // 2
    return jnp.where(
        lower_lanes(values.shape, half),
        pltpu.roll(values, width - half, 1),
        pltpu.roll(values, half, 1),
    )


def rotated_heads(raw, query_gain, key_gain, cosine, sine, head_dim):
    width = 2 * head_dim
    queries = raw[:, :width]
    keys = raw[:, width:]
    query_norm = lax.rsqrt(pair_scale(queries * queries, head_dim) + norm_eps)
    key_norm = lax.rsqrt(pair_scale(keys * keys, head_dim) + norm_eps)
    query_hat = queries * query_norm
    key_hat = keys * key_norm
    scaled = query_hat * query_gain
    query_rot = scaled * cosine + swap_halves(scaled, head_dim) * sine
    scaled = key_hat * key_gain
    key_rot = scaled * cosine + swap_halves(scaled, head_dim) * sine
    lower = lower_lanes(keys.shape, head_dim)
    key_twice = jnp.where(lower, key_rot, pltpu.roll(key_rot, head_dim, 1))
    value_twice = jnp.where(lower, pltpu.roll(keys, head_dim, 1), keys)
    return query_hat, query_norm, key_hat, key_norm, query_rot, key_twice, value_twice


def stack_heads(values, head_dim):
    lower = lower_lanes(values.shape, head_dim)
    zero = jnp.zeros_like(values)
    return jnp.concatenate(
        [jnp.where(lower, values, zero), jnp.where(lower, zero, values)], axis=0
    )


def join_heads(stacked, head_dim):
    rows = stacked.shape[0] // 2
    lower = lower_lanes((rows, stacked.shape[1]), head_dim)
    return jnp.where(lower, stacked[:rows], stacked[rows:])


def allowed_pairs(doc_column, doc_row, first, rows, span):
    row_index = first + lax.broadcasted_iota(jnp.int32, (rows, span), 0)
    key_index = lax.broadcasted_iota(jnp.int32, (rows, span), 1)
    return (doc_column == doc_row) & (key_index <= row_index)


def dot_last(left, right):
    return lax.dot_general(left, right, contract_last, preferred_element_type=jnp.float32)


def dot_first(left, right):
    return lax.dot_general(left, right, contract_first, preferred_element_type=jnp.float32)


def dot_plain(left, right):
    return jnp.dot(left, right, preferred_element_type=jnp.float32)


def scalar_spec():
    return pl.BlockSpec(memory_space=pltpu.SMEM)


def whole_spec():
    return pl.BlockSpec(memory_space=pltpu.VMEM)


def any_spec():
    return pl.BlockSpec(memory_space=pltpu.HBM)


def in_hbm(values):
    return [pltpu.with_memory_space_constraint(value, pltpu.HBM) for value in values]


def start_copies(copies, sems, first=0):
    handles = [
        pltpu.make_async_copy(source, target, sems.at[first + at])
        for at, (source, target) in enumerate(copies)
    ]
    for handle in handles:
        handle.start()
    return handles


def pack_heads(w_query, key_weight, value_weight, places, head_dim):
    rows = w_query.shape[0]
    width = 2 * head_dim

    def kernel(place_ref, query_ref, key_ref, value_ref, *out_refs):
        shard = place_ref[0]
        core = place_ref[1]
        for step, out_ref in enumerate(out_refs):
            other = shard ^ step
            out_ref[:, :width] = query_ref[
                :, pl.ds(pl.multiple_of((2 * other + core) * width, width), width)
            ]
            lanes = pl.ds(pl.multiple_of(other * width, width), width)
            keys = key_ref[:, lanes].astype(jnp.float32)
            values = value_ref[:, lanes].astype(jnp.float32)
            lower = lower_lanes(keys.shape, head_dim)
            first = jnp.where(lower, keys, pltpu.roll(values, head_dim, 1))
            second = jnp.where(lower, pltpu.roll(keys, head_dim, 1), values)
            out_ref[:, width:] = jnp.where(core == 0, first, second).astype(jnp.bfloat16)

    return pl.pallas_call(
        kernel,
        name="pack_heads",
        in_specs=[scalar_spec()] + [whole_spec()] * 3,
        out_shape=(jax.ShapeDtypeStruct((rows, 2 * width), jnp.bfloat16),) * 4,
    )(places, w_query, key_weight, value_weight)


def attention_forward(head_dim, block):
    score_scale = head_dim ** (-0.5)
    assert score_scale == 2.0 ** round(math.log2(score_scale))
    width = 2 * head_dim

    def kernel(
        place_ref, gain_ref, piece_0, piece_1, piece_2, piece_3, query_gain_ref,
        key_gain_ref, cos_hbm, sin_hbm, doc_col_hbm, doc_row_ref, *refs,
    ):
        x_refs = refs[:8]
        mix_ref, normed_out, raw_out, lse_out, weight_out = refs[8:13]
        query_scr, key_scr, value_scr, x_scr, sems = refs[13:18]
        cos_ref, sin_ref, doc_col_ref, normed_ref, raw_ref, lse_ref, weight_ref = refs[18:]
        total = cos_ref.shape[0]
        shard = place_ref[0]
        rank = 2 * shard + place_ref[1]
        piece_rows = piece_0.shape[0]
        own_rows = total // 8
        copies = []
        for step, piece in enumerate((piece_0, piece_1, piece_2, piece_3)):
            first = pl.multiple_of((shard ^ step) * piece_rows, piece_rows)
            copies.append((piece, weight_ref.at[pl.ds(first, piece_rows), :]))
        for step, x_ref in enumerate(x_refs):
            copies.append((x_ref, x_scr.at[pl.ds(step * own_rows, own_rows), :]))
        copies += [(cos_hbm, cos_ref), (sin_hbm, sin_ref), (doc_col_hbm, doc_col_ref)]
        handles = start_copies(copies, sems)
        for handle in handles:
            handle.wait()
        outward = start_copies([(weight_ref, weight_out)], sems, len(copies))

        def normalize(step, carry):
            rows = pl.ds(pl.multiple_of(step * own_rows, own_rows), own_rows)
            x = x_scr[rows, :].astype(jnp.float32)
            normed_ref[rows, :] = (x * rms_scale(x) * gain_ref[...]).astype(jnp.bfloat16)
            return carry

        lax.fori_loop(0, 8, normalize, 0)
        for half in range(0, total, 4 * own_rows):
            raw = dot_plain(normed_ref[pl.ds(half, 4 * own_rows), :], weight_ref[...])
            for step in range(4):
                mask = xor_order[half // own_rows + step]
                first = pl.multiple_of((rank ^ mask) * own_rows, own_rows)
                raw_ref[pl.ds(first, own_rows), :] = raw[step * own_rows : (step + 1) * own_rows]
        outward += start_copies(
            [(normed_ref, normed_out), (raw_ref, raw_out)], sems, len(copies) + 1
        )

        def rotate(step, carry):
            rows = pl.ds(pl.multiple_of(step * block, block), block)
            parts = rotated_heads(
                raw_ref[rows, :], query_gain_ref[...], key_gain_ref[...], cos_ref[rows, :],
                sin_ref[rows, :], head_dim,
            )
            query_scr[rows, :] = (parts[4].astype(jnp.bfloat16) * score_scale).astype(jnp.bfloat16)
            key_scr[rows, :] = parts[5].astype(jnp.bfloat16)
            value_scr[rows, :] = parts[6].astype(jnp.bfloat16)
            return carry

        lax.fori_loop(0, total // block, rotate, 0)
        for first in range(0, total, block):
            rows = pl.ds(first, block)
            span = first + block
            stacked = stack_heads(query_scr[rows, :], head_dim)
            allowed = allowed_pairs(
                doc_col_ref[rows, :], doc_row_ref[:, :span], first, block, span
            )
            allowed = jnp.concatenate([allowed, allowed], axis=0)
            scores = dot_last(stacked, key_scr[:span, :])
            powers = jnp.exp(jnp.where(allowed, scores, very_low))
            row_total = jnp.sum(powers, axis=1, keepdims=True)
            probs = (powers * (1.0 / row_total)).astype(jnp.bfloat16)
            mixed = dot_plain(probs, value_scr[:span, :])
            mix_ref[rows, :] = join_heads(mixed, head_dim).astype(jnp.bfloat16)
            lse_ref[pl.ds(2 * first, 2 * block), :] = jnp.log(row_total)
        outward += start_copies([(lse_ref, lse_out)], sems, len(copies) + 3)
        for handle in outward:
            handle.wait()

    def call(places, xs, gain, pieces, query_gain, key_gain, cosine, sine, doc_column, doc_row):
        total, model = cosine.shape[0], xs[0].shape[1]
        return pl.pallas_call(
            kernel,
            name="attention_forward",
            in_specs=[scalar_spec(), whole_spec()]
            + [any_spec()] * 4
            + [whole_spec()] * 2
            + [any_spec()] * 3
            + [whole_spec()]
            + [any_spec()] * 8,
            out_specs=(whole_spec(),) + (any_spec(),) * 4,
            compiler_params=pltpu.CompilerParams(vmem_limit_bytes=32 << 20),
            out_shape=(
                jax.ShapeDtypeStruct((total, width), jnp.bfloat16),
                pltpu.HBM((total, model), jnp.bfloat16),
                pltpu.HBM((total, 2 * width), jnp.float32),
                pltpu.HBM((2 * total, 1), jnp.float32),
                pltpu.HBM((model, 2 * width), jnp.bfloat16),
            ),
            scratch_shapes=[pltpu.VMEM((total, width), jnp.bfloat16)] * 3
            + [
                pltpu.VMEM((total, model), jnp.bfloat16),
                pltpu.SemaphoreType.DMA((19,)),
                pltpu.VMEM((total, width), jnp.float32),
                pltpu.VMEM((total, width), jnp.float32),
                pltpu.VMEM((total, 1), jnp.int32),
                pltpu.VMEM((total, model), jnp.bfloat16),
                pltpu.VMEM((total, 2 * width), jnp.float32),
                pltpu.VMEM((2 * total, 1), jnp.float32),
                pltpu.VMEM((model, 2 * width), jnp.bfloat16),
            ],
        )(
            places, gain, *in_hbm(pieces), query_gain, key_gain,
            *in_hbm((cosine, sine, doc_column)), doc_row, *in_hbm(xs),
        )

    return call


def residual_stage(places, mix_pieces, out_pieces, xs, mlp_gain):
    total, model = 8 * xs[0].shape[0], xs[0].shape[1]
    width = mix_pieces[0].shape[1]
    own_rows = out_pieces[0].shape[0]

    def kernel(place_ref, gain_ref, *refs):
        mix_refs = refs[:8]
        out_refs = refs[8:16]
        x_refs = refs[16:24]
        normed_ref, mixed_out, cols_out, resid_out, hat_out, scale_ref = refs[24:30]
        weight_scr, x_scr, sems, mixed_ref, cols_ref, resid_ref, hat_ref = refs[30:]
        rank = 2 * place_ref[0] + place_ref[1]
        copies = []
        for mask, ref in zip(xor_order, out_refs):
            first = pl.multiple_of((rank ^ mask) * own_rows, own_rows)
            copies.append((ref, weight_scr.at[pl.ds(first, own_rows), :]))
        for step, row_mask in enumerate(xor_order):
            first = pl.multiple_of((rank ^ row_mask) * own_rows, own_rows)
            for mask, ref in zip(xor_order, mix_refs):
                lanes = pl.ds(pl.multiple_of((rank ^ mask) * width, width), width)
                copies.append(
                    (
                        ref.at[pl.ds(first, own_rows), :],
                        mixed_ref.at[pl.ds(step * own_rows, own_rows), lanes],
                    )
                )
        for step, ref in enumerate(x_refs):
            copies.append((ref, x_scr.at[pl.ds(step * own_rows, own_rows), :]))
        handles = start_copies(copies, sems)
        for handle in handles:
            handle.wait()
        cols_ref[...] = weight_scr[:, pl.ds(pl.multiple_of(rank * width, width), width)]
        outward = start_copies(
            [(mixed_ref, mixed_out), (cols_ref, cols_out)], sems, len(copies)
        )
        for first in range(0, total, total // 4):
            rows = pl.ds(first, total // 4)
            resid = x_scr[rows, :].astype(jnp.float32) + dot_last(
                mixed_ref[rows, :], weight_scr[...]
            )
            scale = rms_scale(resid)
            hat = resid * scale
            normed_ref[rows, :] = (hat * gain_ref[...]).astype(jnp.bfloat16)
            if first == 0:
                resid_ref[...] = resid[:own_rows]
                hat_ref[...] = hat[:own_rows]
                scale_ref[...] = scale[:own_rows]
                outward += start_copies(
                    [(resid_ref, resid_out), (hat_ref, hat_out)], sems, len(copies) + 2
                )
        for handle in outward:
            handle.wait()

    return pl.pallas_call(
        kernel,
        name="residual_stage",
        in_specs=[scalar_spec(), whole_spec()] + [any_spec()] * 24,
        out_specs=(whole_spec(),) + (any_spec(),) * 4 + (whole_spec(),),
        compiler_params=pltpu.CompilerParams(vmem_limit_bytes=24 << 20),
        out_shape=(
            jax.ShapeDtypeStruct((total, model), jnp.bfloat16),
            pltpu.HBM((total, model), jnp.bfloat16),
            pltpu.HBM((model, width), jnp.bfloat16),
            pltpu.HBM((own_rows, model), jnp.float32),
            pltpu.HBM((own_rows, model), jnp.float32),
            jax.ShapeDtypeStruct((own_rows, 1), jnp.float32),
        ),
        scratch_shapes=[
            pltpu.VMEM((model, model), jnp.bfloat16),
            pltpu.VMEM((total, model), jnp.bfloat16),
            pltpu.SemaphoreType.DMA((84,)),
            pltpu.VMEM((total, model), jnp.bfloat16),
            pltpu.VMEM((model, width), jnp.bfloat16),
            pltpu.VMEM((own_rows, model), jnp.float32),
            pltpu.VMEM((own_rows, model), jnp.float32),
        ],
    )(places, mlp_gain, *in_hbm((*mix_pieces, *out_pieces, *xs)))


def stack_rows(pieces):
    rows, width = pieces[0].shape

    def kernel(*refs):
        out_ref, sems = refs[-2:]
        handles = start_copies(
            [(ref, out_ref.at[pl.ds(at * rows, rows), :]) for at, ref in enumerate(refs[:-2])],
            sems,
        )
        for handle in handles:
            handle.wait()

    return pl.pallas_call(
        kernel,
        name="stack_rows",
        in_specs=[any_spec()] * len(pieces),
        compiler_params=pltpu.CompilerParams(vmem_limit_bytes=8 << 20),
        scratch_shapes=[pltpu.SemaphoreType.DMA((len(pieces),))],
        out_shape=jax.ShapeDtypeStruct((rows * len(pieces), width), pieces[0].dtype),
    )(*pieces)


def attention_backward(head_dim, block):
    score_scale = head_dim ** (-0.5)
    assert score_scale == 2.0 ** round(math.log2(score_scale))
    width = 2 * head_dim

    def kernel(
        place_ref, raw_ref, mix_ref, out_cols_ref, lse_ref, query_gain_ref,
        key_gain_ref, cos_ref, sin_ref, doc_col_ref, doc_row_ref, normed_ref, *refs,
    ):
        resid_refs = refs[:8]
        grads_out_ref, query_part_ref, key_part_ref, resid_own_ref = refs[8:12]
        refs = refs[12:]
        piece_refs = refs[:8]
        query_scr, key_scr, value_scr, mix_grad_scr, grads_ref, key_sum, value_sum = refs[8:15]
        resid_scr, sems = refs[15:]
        total = raw_ref.shape[0]
        own_rows = total // 8
        rank = 2 * place_ref[0] + place_ref[1]
        handles = start_copies(
            [
                (ref, resid_scr.at[pl.ds(step * own_rows, own_rows), :])
                for step, ref in enumerate(resid_refs)
            ],
            sems,
        )

        def rotate(step, carry):
            rows = pl.ds(pl.multiple_of(step * block, block), block)
            parts = rotated_heads(
                raw_ref[rows, :], query_gain_ref[...], key_gain_ref[...], cos_ref[rows, :],
                sin_ref[rows, :], head_dim,
            )
            query_scr[rows, :] = (parts[4].astype(jnp.bfloat16) * score_scale).astype(jnp.bfloat16)
            key_scr[rows, :] = parts[5].astype(jnp.bfloat16)
            value_scr[rows, :] = parts[6].astype(jnp.bfloat16)
            return carry

        lax.fori_loop(0, total // block, rotate, 0)
        for handle in handles:
            handle.wait()
        resid_own_ref[...] = resid_scr[:, pl.ds(pl.multiple_of(rank * width, width), width)]
        for half in range(0, total, 4 * own_rows):
            mix_grad = dot_plain(
                resid_scr[pl.ds(half, 4 * own_rows), :], out_cols_ref[...]
            ).astype(jnp.bfloat16)
            for step in range(4):
                mask = xor_order[half // own_rows + step]
                first = pl.multiple_of((rank ^ mask) * own_rows, own_rows)
                mix_grad_scr[pl.ds(first, own_rows), :] = mix_grad[
                    step * own_rows : (step + 1) * own_rows
                ]
        query_gain = query_gain_ref[...]
        key_gain = key_gain_ref[...]

        def heads_of(rows):
            return rotated_heads(
                raw_ref[rows, :], query_gain, key_gain, cos_ref[rows, :], sin_ref[rows, :],
                head_dim,
            )

        def unrotated(grad, rows):
            return grad * cos_ref[rows, :] - swap_halves(grad, head_dim) * sin_ref[rows, :]

        def norm_back(upstream, hat, norm, gain):
            scaled = upstream * gain
            return norm * (scaled - hat * pair_scale(scaled * hat, head_dim))

        key_sum[...] = jnp.zeros_like(key_sum)
        value_sum[...] = jnp.zeros_like(value_sum)
        wide = 2 * block

        def query_block(step, query_part):
            first = pl.multiple_of(step * block, block)
            rows = pl.ds(first, block)
            stacked = stack_heads(query_scr[rows, :], head_dim)
            stacked_grad = stack_heads(mix_grad_scr[rows, :], head_dim)
            mixed = mix_ref[rows, :].astype(jnp.float32)
            delta = jnp.sum(
                stacked_grad.astype(jnp.float32) * jnp.concatenate([mixed, mixed], axis=0),
                axis=1,
                keepdims=True,
            )
            lse = lse_ref[pl.ds(pl.multiple_of(2 * first, 2 * block), 2 * block), :]
            doc_column = doc_col_ref[rows, :]

            def key_block(at, rotated):
                begin = pl.multiple_of(at * wide, wide)
                keys = pl.ds(begin, wide)
                allowed = allowed_pairs(
                    doc_column, doc_row_ref[:, keys], first - begin, block, wide
                )
                allowed = jnp.concatenate([allowed, allowed], axis=0)
                scores = dot_last(stacked, key_scr[keys, :])
                probs = jnp.exp(jnp.where(allowed, scores - lse, very_low))
                prob_grad = dot_last(stacked_grad, value_scr[keys, :])
                score_grad = (probs * (prob_grad - delta)).astype(jnp.bfloat16)
                key_sum[keys, :] += dot_first(score_grad, stacked)
                value_sum[keys, :] += dot_first(probs.astype(jnp.bfloat16), stacked_grad)
                return rotated + dot_plain(score_grad, key_scr[keys, :])

            rotated = lax.fori_loop(
                0, step // 2 + 1, key_block, jnp.zeros((2 * block, width), jnp.float32)
            )
            query_hat, query_norm = heads_of(rows)[:2]
            straight = unrotated(join_heads(rotated, head_dim) * score_scale, rows)
            grads_ref[rows, :width] = norm_back(
                straight, query_hat, query_norm, query_gain
            ).astype(jnp.bfloat16)
            return query_part + jnp.sum(straight * query_hat, axis=0, keepdims=True)

        zero_part = jnp.zeros((1, width), jnp.float32)
        query_part = lax.fori_loop(0, total // block, query_block, zero_part)

        def finish_keys(step, key_part):
            rows = pl.ds(pl.multiple_of(step * block, block), block)
            key_hat, key_norm = heads_of(rows)[2:4]
            summed = key_sum[rows, :]
            summed = summed + pltpu.roll(summed, head_dim, 1)
            values = value_sum[rows, :]
            values = values + pltpu.roll(values, head_dim, 1)
            straight = unrotated(summed, rows)
            key_grad = norm_back(straight, key_hat, key_norm, key_gain)
            lower = lower_lanes(key_grad.shape, head_dim)
            grads_ref[rows, width:] = jnp.where(lower, key_grad, values).astype(jnp.bfloat16)
            return key_part + jnp.sum(straight * key_hat, axis=0, keepdims=True)

        key_part = lax.fori_loop(0, total // block, finish_keys, zero_part)
        query_part_ref[...] = query_part
        key_part_ref[...] = key_part
        for step, mask in enumerate(xor_order):
            first = pl.multiple_of((rank ^ mask) * own_rows, own_rows)
            grads_out_ref[pl.ds(step * own_rows, own_rows), :] = grads_ref[
                pl.ds(first, own_rows), :
            ]
        for mask, piece_ref in enumerate(piece_refs):
            lanes = pl.ds(pl.multiple_of((rank ^ mask) * width, width), width)
            piece_ref[...] = dot_first(normed_ref[:, lanes], grads_out_ref[...]).astype(
                jnp.bfloat16
            )

    def call(
        places, raw, mix, resids, out_cols, lse, query_gain, key_gain, cosine, sine, doc_col,
        doc_row, normed,
    ):
        total = raw.shape[0]
        return pl.pallas_call(
            kernel,
            name="attention_backward",
            in_specs=[scalar_spec()] + [whole_spec()] * 11 + [any_spec()] * 8,
            compiler_params=pltpu.CompilerParams(vmem_limit_bytes=36 << 20),
            out_shape=(
                jax.ShapeDtypeStruct((total, 2 * width), jnp.bfloat16),
                jax.ShapeDtypeStruct((1, width), jnp.float32),
                jax.ShapeDtypeStruct((1, width), jnp.float32),
                jax.ShapeDtypeStruct((total, width), jnp.bfloat16),
            )
            + (jax.ShapeDtypeStruct((width, 2 * width), jnp.bfloat16),) * 8,
            scratch_shapes=[pltpu.VMEM((total, width), jnp.bfloat16)] * 4
            + [pltpu.VMEM((total, 2 * width), jnp.bfloat16)]
            + [pltpu.VMEM((total, width), jnp.float32)] * 2
            + [pltpu.VMEM((total, normed.shape[1]), jnp.bfloat16), pltpu.SemaphoreType.DMA((8,))],
        )(
            places, raw, mix, out_cols, lse, query_gain, key_gain, cosine, sine, doc_col,
            doc_row, normed, *in_hbm(resids),
        )

    return call


def unpack_heads(places, summed, head_dim):
    rows = summed.shape[0]
    width = 2 * head_dim
    model = 8 * width

    def kernel(place_ref, sum_ref, query_ref, key_ref, value_ref, out_ref):
        shard = place_ref[0]
        core = place_ref[1]
        for step in range(4):
            other = shard ^ step
            first = sum_ref[:, pl.ds(4 * step * width, 2 * width)].astype(jnp.float32)
            second = sum_ref[:, pl.ds((4 * step + 2) * width, 2 * width)].astype(jnp.float32)
            even = jnp.where(core == 0, first, second)
            odd = jnp.where(core == 0, second, first)
            query_ref[:, pl.ds(pl.multiple_of(2 * other * width, width), width)] = even[:, :width]
            query_ref[:, pl.ds(pl.multiple_of((2 * other + 1) * width, width), width)] = odd[
                :, :width
            ]
            even = even[:, width:]
            odd = odd[:, width:]
            lower = lower_lanes(even.shape, head_dim)
            lanes = pl.ds(pl.multiple_of(other * width, width), width)
            key_ref[:, lanes] = jnp.where(lower, even, pltpu.roll(odd, head_dim, 1))
            value_ref[:, lanes] = jnp.where(lower, pltpu.roll(even, head_dim, 1), odd)
        out_ref[...] = sum_ref[:, 2 * model :].astype(jnp.float32)

    return pl.pallas_call(
        kernel,
        name="unpack_heads",
        in_specs=[scalar_spec(), whole_spec()],
        out_shape=(
            jax.ShapeDtypeStruct((rows, model), jnp.float32),
            jax.ShapeDtypeStruct((rows, model // 2), jnp.float32),
            jax.ShapeDtypeStruct((rows, model // 2), jnp.float32),
            jax.ShapeDtypeStruct((rows, summed.shape[1] - 2 * model), jnp.float32),
        ),
    )(places, summed)


def heads_body(
    tokens_in,
    doc_lengths,
    attn_gain,
    w_query,
    key_weight,
    value_weight,
    w_output,
    query_norm_gain,
    key_norm_gain,
    mlp_gain,
    w_gate,
    w_up,
    w_down,
    out_grad,
):
    row_count, model_width = tokens_in.shape
    head_dim = query_norm_gain.shape[0]
    total = row_count * 8
    half_rows = total // 2
    block = 256
    core = lax.axis_index("seq")
    shard = lax.axis_index("shard")
    places = jnp.stack([shard, core]).astype(jnp.int32)

    x_near = gather_near(tokens_in)
    head_pieces = pack_heads(w_query, key_weight, value_weight, places, head_dim)
    head_pieces = [head_pieces[0]] + [
        group_swap(head_pieces[step], 2 * step) for step in (1, 2, 3)
    ]
    x_far = gather_far(x_near)
    x_pieces = x_near + x_far

    out_near = lax.dynamic_slice_in_dim(w_output, core * row_count, row_count)
    out_local = lax.dynamic_slice_in_dim(w_output, (1 - core) * row_count, row_count)
    out_own = after(out_near, x_near[1:])
    out_near = [out_own]
    for mask in (2, 4, 6):
        out_near.append(group_swap(out_own, mask))
    out_pieces = out_near + [out_local] + gather_far(out_near[1:])

    index = jnp.arange(total, dtype=jnp.int32)
    docs, offsets = doc_info(doc_lengths[0], index)
    half_dim = head_dim // 2
    inverse_freq = rope_base ** (-(jnp.arange(half_dim, dtype=jnp.float32) * 2.0 / head_dim))
    angles = offsets.astype(jnp.float32)[:, None] * jnp.tile(inverse_freq, 4)[None, :]
    cosine = jnp.cos(angles)
    sine = jnp.where(lower_lanes(angles.shape, half_dim), -1.0, 1.0) * jnp.sin(angles)
    doc_column = docs[:, None]
    doc_row = docs[None, :]
    query_gain = jnp.concatenate([query_norm_gain] * 2)[None, :]
    key_gain = jnp.concatenate([key_norm_gain] * 2)[None, :]

    mix, normed, raw, lse, head_weight = attention_forward(head_dim, block)(
        places, x_pieces, attn_gain[None, :], head_pieces, query_gain, key_gain, cosine, sine,
        doc_column, doc_row,
    )
    mix_near = gather_near(mix)
    mix_far = gather_far(mix_near)
    grad_near = gather_near(after(out_grad, mix_near[1:]))
    grad_all = stack_rows(grad_near + gather_far(grad_near))

    normed_mid, mix_all, out_cols, own_resid, own_hat, own_scale = residual_stage(
        places, mix_near + mix_far, out_pieces, x_pieces, mlp_gain[None, :]
    )

    hidden_rows = w_gate.shape[0] // 2

    def own_rows(weight):
        return lax.dynamic_slice_in_dim(weight, core * hidden_rows, hidden_rows)

    gate_rows = own_rows(w_gate)
    up_rows = own_rows(w_up)
    down_rows = own_rows(w_down)
    gate = dot_last(normed_mid, gate_rows)
    up = dot_last(normed_mid, up_rows)
    grad_hidden = dot_last(grad_all, down_rows)
    gate_sig = jax.nn.sigmoid(gate)
    hidden = (gate * gate_sig * up).astype(jnp.bfloat16)
    gate_grad = (grad_hidden * up * gate_sig * (1.0 + gate * (1.0 - gate_sig))).astype(jnp.bfloat16)
    up_grad = (grad_hidden * gate * gate_sig).astype(jnp.bfloat16)

    def mid_part(first):
        rows = slice(first, first + half_rows)
        return dot_plain(gate_grad[rows], gate_rows) + dot_plain(up_grad[rows], up_rows)

    mlp_grads = jnp.concatenate(
        [
            dot_first(hidden, grad_all).astype(jnp.bfloat16),
            dot_first(gate_grad, normed_mid).astype(jnp.bfloat16),
            dot_first(up_grad, normed_mid).astype(jnp.bfloat16),
        ],
        axis=0,
    )
    mlp_sums = lax.psum(mlp_grads, "rep").astype(jnp.float32)

    gate_grad, up_grad = after((gate_grad, up_grad), mlp_grads)
    grad_mid = scatter_sum(mid_part(0), mid_part(half_rows))
    grad_resid = out_grad.astype(jnp.float32) + root_mean_backward(
        own_hat, own_scale, mlp_gain, grad_mid
    )
    mlp_gain_part = jnp.sum(grad_mid * own_hat, axis=0)
    resid_near = gather_near(grad_resid.astype(jnp.bfloat16))
    resid_pieces = resid_near + gather_far(resid_near)

    act_out = own_resid + scatter_sum(
        dot_plain(hidden[:half_rows], down_rows), dot_plain(hidden[half_rows:], down_rows)
    )

    backward = attention_backward(head_dim, block)(
        places, raw, mix, resid_pieces, out_cols, lse, query_gain, key_gain, cosine, sine,
        doc_column, doc_row, normed,
    )
    head_grads, query_part, key_part, resid_own = backward[:4]
    weight_pieces = backward[4:]
    weight_pieces = [weight_pieces[0]] + [
        group_swap(weight_pieces[mask], mask) for mask in range(1, 8)
    ]
    out_grads = dot_first(resid_own, mix_all).astype(jnp.bfloat16)
    grad_in_norm = scatter_sum(
        dot_last(head_grads[:half_rows], head_weight),
        dot_last(head_grads[half_rows:], head_weight),
    )
    own_x = tokens_in.astype(jnp.float32)
    own_norm = rms_scale(own_x)
    x_hat = own_x * own_norm
    in_grad = grad_resid + root_mean_backward(x_hat, own_norm, attn_gain, grad_in_norm)
    attn_gain_part = jnp.sum(grad_in_norm * x_hat, axis=0)
    query_gain_part = query_part[0, :head_dim] + query_part[0, head_dim:]
    gains = sum_everywhere(
        jnp.concatenate(
            [attn_gain_part, mlp_gain_part, query_gain_part, key_part[0, :head_dim]]
        )[None, :]
    )[0]
    attn_grads = rep_halving_sum(
        jnp.concatenate(weight_pieces + [out_grads], axis=1), grad_in_norm, gains
    )
    grad_query, grad_key, grad_value, grad_output = unpack_heads(places, attn_grads, head_dim)
    return (
        act_out,
        in_grad,
        gains[:model_width],
        grad_query,
        grad_key,
        grad_value,
        grad_output,
        gains[2 * model_width : 2 * model_width + head_dim],
        gains[2 * model_width + head_dim :],
        gains[model_width : 2 * model_width],
        mlp_sums[hidden_rows : 2 * hidden_rows],
        mlp_sums[2 * hidden_rows :],
        mlp_sums[:hidden_rows],
    )


def local_by_heads(*arrays):
    return heads_body(*arrays)


def solution(mesh):
    placed = (
        P(("rep", "shard", "seq"), None),
        P("rep", None),
        P(),
        P("shard", None),
        P("shard", None),
        P("shard", None),
        P("shard", None),
        P(),
        P(),
        P(),
        P("shard", None),
        P("shard", None),
        P("shard", None),
        P(("rep", "shard", "seq"), None),
    )
    sizes = dict(mesh.shape)
    by_heads = sizes["rep"] == 4 and sizes["shard"] == 4 and sizes["seq"] == 2
    return jax.shard_map(
        local_by_heads if by_heads else local,
        mesh=mesh,
        in_specs=placed,
        out_specs=(
            P(("rep", "shard", "seq"), None),
            P(("rep", "shard", "seq"), None),
            P(),
            P(("shard", "seq"), None),
            P(("shard", "seq"), None),
            P(("shard", "seq"), None),
            P(("shard", "seq"), None),
            P(),
            P(),
            P(),
            P(("shard", "seq"), None),
            P(("shard", "seq"), None),
            P(("shard", "seq"), None),
        ),
        check_vma=False,
    )
```

profile of v0, /device:TPU:0, one launch (start us, length us, event | category | flops | bytes accessed | tf_op | source)
XLA Modules:
  0.0 293.9 jit_solution(16836039829711606112)
XLA Ops:
  7.8 3.5 %collective-permute-start.5 = (bf16[128,1024]{1,0:T(8,128)(2,1)}, bf16[128,1024]{1,0:T(8,128)(2,1)S(1)}, u32[]{:S(2)}, u32[]{:S(2)}) collective-permute-start(bf16[128,1024]{1,0:T(8,128)(2,1)} %refs_16_.1), channel_id=1, source_target_pairs={{0,6},{1,7},{2,4},{3,5},{4,2},{5,3},{6,0},{7,1},{8,14},{9,15},{10,... | collective-permute-start | bytes 786440 | tf_op jit(solution)/shard_map/ppermute | solution.py:445
  12.6 2.2 pack_heads.1
  14.8 1.9 collective-permute-start
  18.4 8.9 %collective-permute-done.piece_1 = bf16[256,256]{1,0:T(8,128)(2,1)} collective-permute-done((bf16[256,256]{1,0:T(8,128)(2,1)}, bf16[256,256]{1,0:T(8,128)(2,1)}, u32[]{:S(2)}, u32[]{:S(2)}) %collective-permute-start) | collective-permute-done | bytes 131104 | tf_op jit(solution)/shard_map/ppermute | solution.py:445
  28.2 3.0 %fusion.31 = (f32[1024,128]{1,0:T(8,128)}, f32[1024,128]{1,0:T(8,128)}) fusion(s32[128]{0:T(128)S(1)} %get-tuple-element.126, s32[128]{0:T(128)S(1)} %get-tuple-element.127, f32[128]{0:T(128)S(1)} %mul.140, f32[1024]{0:T(1024)S(1)} %subtract_convert_fusion, pred[128]{0:T(512)(128)(4,1)S(1)} %compare_and_fusion), kind=kLoop, calls=%fused_computation.50 | loop fusion | flops 655360 | bytes 1054336 | tf_op jit(solution)/shard_map/mul | solution.py:1114
  35.7 1.8 constant_dynamic-slice_fusion.4
  37.4 1.9 collective-permute-done.2.piece_3
  39.3 2.3 collective-permute-start.19
  42.9 10.2 %attention_forward.1 = (bf16[1024,128]{1,0:T(8,128)(2,1)S(1)}, bf16[1024,1024]{1,0:T(8,128)(2,1)}, f32[1024,256]{1,0:T(8,128)}, f32[2048,1]{1,0:T(8,128)}, bf16[1024,256]{1,0:T(8,128)(2,1)}) custom-call(s32[2]{0:T(128)S(1)} %copy-done.13, f32[1,1024]{1,0:T(1,128)S(1)} %bitcast.40, bf16[256,256]{1,0:T(8,128)(2,1)} %get-tuple-element.52.piece_0, ...), custom_call_target="tpu_custom_call" | custom-call | tf_op jit(solution)/shard_map/attention_forward/pallas_call | solution.py:720
  53.1 2.4 collective-permute-start.12
  57.2 6.2 %collective-permute-done.12.refs_3_ = bf16[1024,128]{1,0:T(8,128)(2,1)} collective-permute-done((bf16[1024,128]{1,0:T(8,128)(2,1)S(1)}, bf16[1024,128]{1,0:T(8,128)(2,1)}, u32[]{:S(2)}, u32[]{:S(2)}) %collective-permute-start.12) | collective-permute-done | bytes 262176 | tf_op jit(solution)/shard_map/ppermute | solution.py:445
  63.4 3.3 %collective-permute-done.11.refs_2_ = bf16[1024,128]{1,0:T(8,128)(2,1)} collective-permute-done((bf16[1024,128]{1,0:T(8,128)(2,1)S(1)}, bf16[1024,128]{1,0:T(8,128)(2,1)}, u32[]{:S(2)}, u32[]{:S(2)}) %collective-permute-start.11) | collective-permute-done | bytes 262176 | tf_op jit(solution)/shard_map/ppermute | solution.py:445
  67.3 1.8 collective-permute-start.29
  72.2 5.3 %collective-permute-done.29.refs_3_ = bf16[128,1024]{1,0:T(8,128)(2,1)S(1)} collective-permute-done((bf16[128,1024]{1,0:T(8,128)(2,1)S(1)}, bf16[128,1024]{1,0:T(8,128)(2,1)S(1)}, u32[]{:S(2)}, u32[]{:S(2)}) %collective-permute-start.29) | collective-permute-done | bytes 262176 | tf_op jit(solution)/shard_map/ppermute | solution.py:445
  77.5 5.0 %collective-permute-done.28.refs_2_ = bf16[128,1024]{1,0:T(8,128)(2,1)S(1)} collective-permute-done((bf16[128,1024]{1,0:T(8,128)(2,1)S(1)}, bf16[128,1024]{1,0:T(8,128)(2,1)S(1)}, u32[]{:S(2)}, u32[]{:S(2)}) %collective-permute-start.28) | collective-permute-done | bytes 262176 | tf_op jit(solution)/shard_map/ppermute | solution.py:445
  82.6 8.0 %residual_stage.1 = (bf16[1024,1024]{1,0:T(8,128)(2,1)S(1)}, bf16[1024,1024]{1,0:T(8,128)(2,1)}, bf16[1024,128]{1,0:T(8,128)(2,1)}, f32[128,1024]{1,0:T(8,128)},...) custom-call(s32[2]{0:T(128)S(1)} %copy-done.13, f32[1,1024]{1,0:T(1,128)S(1)} %bitcast.39, bf16[1024,128]{1,0:T(8,128)(2,1)} %copy-done.6, ...), custom_call_target="tpu_custom_call" | custom-call | tf_op jit(solution)/shard_map/residual_stage/pallas_call | solution.py:811
  94.6 2.3 multiply_convert_fusion
  101.2 2.0 pad_maximum_fusion
  103.2 2.6 fusion.10
  105.8 2.0 add_convert_fusion
  108.3 2.6 fusion.12
  114.7 1.5 collective-permute-start.37
  118.1 4.6 %collective-permute-done.35 = bf16[128,1024]{1,0:T(8,128)(2,1)S(1)} collective-permute-done((bf16[128,1024]{1,0:T(8,128)(2,1)S(1)}, bf16[128,1024]{1,0:T(8,128)(2,1)S(1)}, u32[]{:S(2)}, u32[]{:S(2)}) %collective-permute-start.35) | collective-permute-done | bytes 262176 | tf_op jit(solution)/shard_map/ppermute | solution.py:445
  122.7 5.8 %collective-permute-done.37 = bf16[128,1024]{1,0:T(8,128)(2,1)S(1)} collective-permute-done((bf16[128,1024]{1,0:T(8,128)(2,1)S(1)}, bf16[128,1024]{1,0:T(8,128)(2,1)S(1)}, u32[]{:S(2)}, u32[]{:S(2)}) %collective-permute-start.37) | collective-permute-done | bytes 262176 | tf_op jit(solution)/shard_map/ppermute | solution.py:445
  136.1 5.4 %collective-permute-done.40.refs_3_ = bf16[128,1024]{1,0:T(8,128)(2,1)S(1)} collective-permute-done((bf16[128,1024]{1,0:T(8,128)(2,1)S(1)}, bf16[128,1024]{1,0:T(8,128)(2,1)S(1)}, u32[]{:S(2)}, u32[]{:S(2)}) %collective-permute-start.40) | collective-permute-done | bytes 262176 | tf_op jit(solution)/shard_map/ppermute | solution.py:445
  141.6 3.7 %collective-permute-done.39.refs_2_ = bf16[128,1024]{1,0:T(8,128)(2,1)S(1)} collective-permute-done((bf16[128,1024]{1,0:T(8,128)(2,1)S(1)}, bf16[128,1024]{1,0:T(8,128)(2,1)S(1)}, u32[]{:S(2)}, u32[]{:S(2)}) %collective-permute-start.39) | collective-permute-done | bytes 262176 | tf_op jit(solution)/shard_map/ppermute | solution.py:445
  150.1 15.1 %attention_backward.1 = (bf16[1024,256]{1,0:T(8,128)(2,1)S(1)}, f32[1,128]{1,0:T(1,128)S(1)}, f32[1,128]{1,0:T(1,128)S(1)}, bf16[1024,128]{1,0:T(8,128)(2,1)S(1)...) custom-call(s32[2]{0:T(128)S(1)} %copy-done.13, ...), custom_call_target="tpu_custom_call" | custom-call | tf_op jit(solution)/shard_map/attention_backward/pallas_call | solution.py:1004
  168.6 2.4 collective-permute-done.55
  173.3 2.0 collective-permute-done.57
  175.3 2.3 collective-permute-start.59
  178.2 2.3 collective-permute-done.59
  180.5 2.0 collective-permute-done.60
  184.6 1.5 collective-permute-start.48
  187.8 4.8 %collective-permute-done.46 = bf16[128,1024]{1,0:T(8,128)(2,1)S(1)} collective-permute-done((bf16[128,1024]{1,0:T(8,128)(2,1)S(1)}, bf16[128,1024]{1,0:T(8,128)(2,1)S(1)}, u32[]{:S(2)}, u32[]{:S(2)}) %collective-permute-start.46) | collective-permute-done | bytes 262176 | tf_op jit(solution)/shard_map/ppermute | solution.py:445
  193.8 4.3 %collective-permute-done.48 = bf16[128,1024]{1,0:T(8,128)(2,1)S(1)} collective-permute-done((bf16[128,1024]{1,0:T(8,128)(2,1)S(1)}, bf16[128,1024]{1,0:T(8,128)(2,1)S(1)}, u32[]{:S(2)}, u32[]{:S(2)}) %collective-permute-start.48) | collective-permute-done | bytes 262176 | tf_op jit(solution)/shard_map/ppermute | solution.py:445
  198.1 1.7 collective-permute-start.61
  202.1 3.1 %collective-permute-done.25 = bf16[128,1024]{1,0:T(8,128)(2,1)} collective-permute-done((bf16[128,1024]{1,0:T(8,128)(2,1)}, bf16[128,1024]{1,0:T(8,128)(2,1)}, u32[]{:S(2)}, u32[]{:S(2)}) %collective-permute-start.25) | collective-permute-done | bytes 262176 | tf_op jit(solution)/shard_map/ppermute | solution.py:445
  205.2 2.6 fusion.50
  207.8 31.0 %collective-permute-done.61 = bf16[64,3072]{1,0:T(8,128)(2,1)} collective-permute-done((bf16[64,3072]{1,0:T(8,128)(2,1)}, bf16[64,3072]{1,0:T(8,128)(2,1)}, u32[]{:S(2)}, u32[]{:S(2)}) %collective-permute-start.61) | collective-permute-done | bytes 393248 | tf_op jit(solution)/shard_map/ppermute | solution.py:449
  240.9 1.6 collective-permute-done.50
  243.3 3.0 %collective-permute-done.51 = f32[1,2176]{1,0:T(1,128)S(1)} collective-permute-done((f32[1,2176]{1,0:T(1,128)S(1)}, f32[1,2176]{1,0:T(1,128)S(1)}, u32[]{:S(2)}, u32[]{:S(2)}) %collective-permute-start.51) | collective-permute-done | bytes 8736 | tf_op jit(solution)/shard_map/ppermute | solution.py:445
  246.4 3.6 %collective-permute-done.52 = f32[1,2176]{1,0:T(1,128)S(1)} collective-permute-done((f32[1,2176]{1,0:T(1,128)S(1)}, f32[1,2176]{1,0:T(1,128)S(1)}, u32[]{:S(2)}, u32[]{:S(2)}) %collective-permute-start.52) | collective-permute-done | bytes 8736 | tf_op jit(solution)/shard_map/ppermute | solution.py:449
  252.6 1.6 collective-permute-start.62
  255.4 6.8 %collective-permute-done.62 = bf16[32,3072]{1,0:T(8,128)(2,1)S(1)} collective-permute-done((bf16[32,3072]{1,0:T(8,128)(2,1)S(1)}, bf16[32,3072]{1,0:T(8,128)(2,1)S(1)}, u32[]{:S(2)}, u32[]{:S(2)}) %collective-permute-start.62) | collective-permute-done | bytes 196640 | tf_op jit(solution)/shard_map/ppermute | solution.py:449
  262.9 9.5 %collective-permute-done.63 = bf16[32,3072]{1,0:T(8,128)(2,1)S(1)} collective-permute-done((bf16[32,3072]{1,0:T(8,128)(2,1)S(1)}, bf16[32,3072]{1,0:T(8,128)(2,1)S(1)}, u32[]{:S(2)}, u32[]{:S(2)}) %collective-permute-start.63) | collective-permute-done | bytes 196640 | tf_op jit(solution)/shard_map/ppermute | solution.py:449
  272.6 5.2 %fusion.66 = (f32[576,1024]{1,0:T(8,128)}, f32[576,1024]{1,0:T(8,128)}, f32[576,1024]{1,0:T(8,128)}) fusion(bf16[1728,1024]{1,0:T(8,128)(2,1)} %all-reduce.2.cloned.1.call-done), kind=kLoop, calls=%fused_computation.133 | loop fusion | bytes 14155776 | tf_op jit(solution)/shard_map/slice | solution.py:1218
  277.8 5.8 %collective-permute-done.64 = bf16[64,3072]{1,0:T(8,128)(2,1)S(1)} collective-permute-done((bf16[64,3072]{1,0:T(8,128)(2,1)S(1)}, bf16[64,3072]{1,0:T(8,128)(2,1)S(1)}, u32[]{:S(2)}, u32[]{:S(2)}) %collective-permute-start.64) | collective-permute-done | bytes 393248 | tf_op jit(solution)/shard_map/ppermute | solution.py:449
  284.6 2.4 unpack_heads.1
  (273 shorter events, 64.0 us)
Async XLA Ops:
  7.2 265.4 %all-reduce.2.cloned.1.call-start = ((), (), s32[]{:S(2)}) async-start(), calls=%async_computation | async-start | bytes 7077888 | tf_op jit(solution)/shard_map/psum | solution.py:1161
  7.3 34.3 %collective-permute-start.6 = (bf16[128,1024]{1,0:T(8,128)(2,1)}, bf16[128,1024]{1,0:T(8,128)(2,1)S(1)}, u32[]{:S(2)}, u32[]{:S(2)}) collective-permute-start(bf16[128,1024]{1,0:T(8,128)(2,1)} %refs_16_.1), channel_id=1, source_target_pairs={{0,1},{1,0},{2,3},{3,2},{4,5},{5,4},{6,7},{7,6},{8,9},{9,8},{10,11... | collective-permute-start | bytes 786440 | tf_op jit(solution)/shard_map/ppermute | solution.py:445
  7.8 19.8 %collective-permute-start.5 = (bf16[128,1024]{1,0:T(8,128)(2,1)}, bf16[128,1024]{1,0:T(8,128)(2,1)S(1)}, u32[]{:S(2)}, u32[]{:S(2)}) collective-permute-start(bf16[128,1024]{1,0:T(8,128)(2,1)} %refs_16_.1), channel_id=1, source_target_pairs={{0,6},{1,7},{2,4},{3,5},{4,2},{5,3},{6,0},{7,1},{8,14},{9,15},{10,... | collective-permute-start | bytes 786440 | tf_op jit(solution)/shard_map/ppermute | solution.py:445
  11.3 16.3 %collective-permute-start.4 = (bf16[128,1024]{1,0:T(8,128)(2,1)}, bf16[128,1024]{1,0:T(8,128)(2,1)S(1)}, u32[]{:S(2)}, u32[]{:S(2)}) collective-permute-start(bf16[128,1024]{1,0:T(8,128)(2,1)} %refs_16_.1), channel_id=1, source_target_pairs={{0,4},{1,5},{2,6},{3,7},{4,0},{5,1},{6,2},{7,3},{8,12},{9,13},{10,... | collective-permute-start | bytes 786440 | tf_op jit(solution)/shard_map/ppermute | solution.py:445
  11.8 16.3 %collective-permute-start.3 = (bf16[128,1024]{1,0:T(8,128)(2,1)}, bf16[128,1024]{1,0:T(8,128)(2,1)S(1)}, u32[]{:S(2)}, u32[]{:S(2)}) collective-permute-start(bf16[128,1024]{1,0:T(8,128)(2,1)} %refs_16_.1), channel_id=1, source_target_pairs={{0,2},{1,3},{2,0},{3,1},{4,6},{5,7},{6,4},{7,5},{8,10},{9,11},{10,... | collective-permute-start | bytes 786440 | tf_op jit(solution)/shard_map/ppermute | solution.py:445
  14.8 12.5 %collective-permute-start = (bf16[256,256]{1,0:T(8,128)(2,1)}, bf16[256,256]{1,0:T(8,128)(2,1)}, u32[]{:S(2)}, u32[]{:S(2)}) collective-permute-start(bf16[256,256]{1,0:T(8,128)(2,1)} %get-tuple-element.53), channel_id=1, source_target_pairs={{0,2},{1,3},{2,0},{3,1},{4,6},{5,7},{6,4},{7,5},{8,10},{9,11},{10,... | collective-permute-start | bytes 393224 | tf_op jit(solution)/shard_map/ppermute | solution.py:445
  27.3 5.2 %collective-permute-start.1 = (bf16[256,256]{1,0:T(8,128)(2,1)}, bf16[256,256]{1,0:T(8,128)(2,1)S(1)}, u32[]{:S(2)}, u32[]{:S(2)}) collective-permute-start(bf16[256,256]{1,0:T(8,128)(2,1)} %get-tuple-element.54), channel_id=1, source_target_pairs={{0,4},{1,5},{2,6},{3,7},{4,0},{5,1},{6,2},{7,3},{8,12},{9,13},{10,... | collective-permute-start | bytes 393224 | tf_op jit(solution)/shard_map/ppermute | solution.py:445
  27.6 14.7 %collective-permute-start.9 = (bf16[128,1024]{1,0:T(8,128)(2,1)S(1)}, bf16[128,1024]{1,0:T(8,128)(2,1)}, u32[]{:S(2)}, u32[]{:S(2)}) collective-permute-start(bf16[128,1024]{1,0:T(8,128)(2,1)S(1)} %collective-permute-done.5.refs_3_.refs_19_), channel_id=1, source_target_pairs={{0,1},{1,0},{2,3},{3,2},{4,5},{5,4},{6,7},{7,6},{8,9},{9,8},{10,11... | collective-permute-start | bytes 786440 | tf_op jit(solution)/shard_map/ppermute | solution.py:445
  27.6 15.2 %collective-permute-start.8 = (bf16[128,1024]{1,0:T(8,128)(2,1)S(1)}, bf16[128,1024]{1,0:T(8,128)(2,1)}, u32[]{:S(2)}, u32[]{:S(2)}) collective-permute-start(bf16[128,1024]{1,0:T(8,128)(2,1)S(1)} %collective-permute-done.4.refs_2_.refs_18_), channel_id=1, source_target_pairs={{0,1},{1,0},{2,3},{3,2},{4,5},{5,4},{6,7},{7,6},{8,9},{9,8},{10,11... | collective-permute-start | bytes 786440 | tf_op jit(solution)/shard_map/ppermute | solution.py:445
  28.1 14.7 %collective-permute-start.7 = (bf16[128,1024]{1,0:T(8,128)(2,1)S(1)}, bf16[128,1024]{1,0:T(8,128)(2,1)}, u32[]{:S(2)}, u32[]{:S(2)}) collective-permute-start(bf16[128,1024]{1,0:T(8,128)(2,1)S(1)} %collective-permute-done.3.refs_1_.refs_17_), channel_id=1, source_target_pairs={{0,1},{1,0},{2,3},{3,2},{4,5},{5,4},{6,7},{7,6},{8,9},{9,8},{10,11... | collective-permute-start | bytes 786440 | tf_op jit(solution)/shard_map/ppermute | solution.py:445
  33.1 6.2 %collective-permute-start.2 = (bf16[256,256]{1,0:T(8,128)(2,1)}, bf16[256,256]{1,0:T(8,128)(2,1)}, u32[]{:S(2)}, u32[]{:S(2)}) collective-permute-start(bf16[256,256]{1,0:T(8,128)(2,1)} %get-tuple-element.55), channel_id=1, source_target_pairs={{0,6},{1,7},{2,4},{3,5},{4,2},{5,3},{6,0},{7,1},{8,14},{9,15},{10,... | collective-permute-start | bytes 393224 | tf_op jit(solution)/shard_map/ppermute | solution.py:445
  39.3 16.8 %collective-permute-start.19 = (bf16[128,1024]{1,0:T(8,128)(2,1)S(1)}, bf16[128,1024]{1,0:T(8,128)(2,1)S(1)}, u32[]{:S(2)}, u32[]{:S(2)}) collective-permute-start(bf16[128,1024]{1,0:T(8,128)(2,1)S(1)} %get-tuple-element.57.refs_8_), channel_id=1, source_target_pairs={{0,6},{1,7},{2,4},{3,5},{4,2},{5,3},{6,0},{7,1},{8,14},{9,15},{10,... | collective-permute-start | bytes 786440 | tf_op jit(solution)/shard_map/ppermute | solution.py:445
  41.6 15.1 %collective-permute-start.18 = (bf16[128,1024]{1,0:T(8,128)(2,1)S(1)}, bf16[128,1024]{1,0:T(8,128)(2,1)S(1)}, u32[]{:S(2)}, u32[]{:S(2)}) collective-permute-start(bf16[128,1024]{1,0:T(8,128)(2,1)S(1)} %get-tuple-element.57.refs_8_), channel_id=1, source_target_pairs={{0,4},{1,5},{2,6},{3,7},{4,0},{5,1},{6,2},{7,3},{8,12},{9,13},{10,... | collective-permute-start | bytes 786440 | tf_op jit(solution)/shard_map/ppermute | solution.py:445
  42.3 14.4 %collective-permute-start.17 = (bf16[128,1024]{1,0:T(8,128)(2,1)S(1)}, bf16[128,1024]{1,0:T(8,128)(2,1)S(1)}, u32[]{:S(2)}, u32[]{:S(2)}) collective-permute-start(bf16[128,1024]{1,0:T(8,128)(2,1)S(1)} %get-tuple-element.57.refs_8_), channel_id=1, source_target_pairs={{0,2},{1,3},{2,0},{3,1},{4,6},{5,7},{6,4},{7,5},{8,10},{9,11},{10,... | collective-permute-start | bytes 786440 | tf_op jit(solution)/shard_map/ppermute | solution.py:445
  53.1 10.3 %collective-permute-start.12 = (bf16[1024,128]{1,0:T(8,128)(2,1)S(1)}, bf16[1024,128]{1,0:T(8,128)(2,1)}, u32[]{:S(2)}, u32[]{:S(2)}) collective-permute-start(bf16[1024,128]{1,0:T(8,128)(2,1)S(1)} %get-tuple-element.56.refs_0_.mix_ref), channel_id=1, source_target_pairs={{0,6},{1,7},{2,4},{3,5},{4,2},{5,3},{6,0},{7,1},{8,14},{9,15},{10,... | collective-permute-start | bytes 786440 | tf_op jit(solution)/shard_map/ppermute | solution.py:445
  55.5 11.2 %collective-permute-start.11 = (bf16[1024,128]{1,0:T(8,128)(2,1)S(1)}, bf16[1024,128]{1,0:T(8,128)(2,1)}, u32[]{:S(2)}, u32[]{:S(2)}) collective-permute-start(bf16[1024,128]{1,0:T(8,128)(2,1)S(1)} %get-tuple-element.56.refs_0_.mix_ref), channel_id=1, source_target_pairs={{0,4},{1,5},{2,6},{3,7},{4,0},{5,1},{6,2},{7,3},{8,12},{9,13},{10,... | collective-permute-start | bytes 786440 | tf_op jit(solution)/shard_map/ppermute | solution.py:445
  56.1 10.6 %collective-permute-start.10 = (bf16[1024,128]{1,0:T(8,128)(2,1)S(1)}, bf16[1024,128]{1,0:T(8,128)(2,1)}, u32[]{:S(2)}, u32[]{:S(2)}) collective-permute-start(bf16[1024,128]{1,0:T(8,128)(2,1)S(1)} %get-tuple-element.56.refs_0_.mix_ref), channel_id=1, source_target_pairs={{0,2},{1,3},{2,0},{3,1},{4,6},{5,7},{6,4},{7,5},{8,10},{9,11},{10,... | collective-permute-start | bytes 786440 | tf_op jit(solution)/shard_map/ppermute | solution.py:445
  56.7 10.6 %collective-permute-start.22 = (bf16[128,1024]{1,0:T(8,128)(2,1)S(1)}, bf16[128,1024]{1,0:T(8,128)(2,1)S(1)}, u32[]{:S(2)}, u32[]{:S(2)}) collective-permute-start(bf16[128,1024]{1,0:T(8,128)(2,1)S(1)} %collective-permute-done.19.refs_11_), channel_id=1, source_target_pairs={{0,1},{1,0},{2,3},{3,2},{4,5},{5,4},{6,7},{7,6},{8,9},{9,8},{10,11... | collective-permute-start | bytes 786440 | tf_op jit(solution)/shard_map/ppermute | solution.py:445
  56.7 10.6 %collective-permute-start.21 = (bf16[128,1024]{1,0:T(8,128)(2,1)S(1)}, bf16[128,1024]{1,0:T(8,128)(2,1)S(1)}, u32[]{:S(2)}, u32[]{:S(2)}) collective-permute-start(bf16[128,1024]{1,0:T(8,128)(2,1)S(1)} %collective-permute-done.18.refs_10_), channel_id=1, source_target_pairs={{0,1},{1,0},{2,3},{3,2},{4,5},{5,4},{6,7},{7,6},{8,9},{9,8},{10,11... | collective-permute-start | bytes 786440 | tf_op jit(solution)/shard_map/ppermute | solution.py:445
  63.4 5.7 %collective-permute-start.20 = (bf16[128,1024]{1,0:T(8,128)(2,1)S(1)}, bf16[128,1024]{1,0:T(8,128)(2,1)S(1)}, u32[]{:S(2)}, u32[]{:S(2)}) collective-permute-start(bf16[128,1024]{1,0:T(8,128)(2,1)S(1)} %collective-permute-done.17.refs_9_), channel_id=1, source_target_pairs={{0,1},{1,0},{2,3},{3,2},{4,5},{5,4},{6,7},{7,6},{8,9},{9,8},{10,11... | collective-permute-start | bytes 786440 | tf_op jit(solution)/shard_map/ppermute | solution.py:445
  67.3 10.2 %collective-permute-start.29 = (bf16[128,1024]{1,0:T(8,128)(2,1)S(1)}, bf16[128,1024]{1,0:T(8,128)(2,1)S(1)}, u32[]{:S(2)}, u32[]{:S(2)}) collective-permute-start(bf16[128,1024]{1,0:T(8,128)(2,1)S(1)} %copy-done.4), channel_id=1, source_target_pairs={{0,6},{1,7},{2,4},{3,5},{4,2},{5,3},{6,0},{7,1},{8,14},{9,15},{10,... | collective-permute-start | bytes 786440 | tf_op jit(solution)/shard_map/ppermute | solution.py:445
  69.1 13.4 %collective-permute-start.28 = (bf16[128,1024]{1,0:T(8,128)(2,1)S(1)}, bf16[128,1024]{1,0:T(8,128)(2,1)S(1)}, u32[]{:S(2)}, u32[]{:S(2)}) collective-permute-start(bf16[128,1024]{1,0:T(8,128)(2,1)S(1)} %copy-done.4), channel_id=1, source_target_pairs={{0,4},{1,5},{2,6},{3,7},{4,0},{5,1},{6,2},{7,3},{8,12},{9,13},{10,... | collective-permute-start | bytes 786440 | tf_op jit(solution)/shard_map/ppermute | solution.py:445
  71.0 11.6 %collective-permute-start.14 = (bf16[1024,128]{1,0:T(8,128)(2,1)}, bf16[1024,128]{1,0:T(8,128)(2,1)}, u32[]{:S(2)}, u32[]{:S(2)}) collective-permute-start(bf16[1024,128]{1,0:T(8,128)(2,1)} %collective-permute-done.10.refs_1_), channel_id=1, source_target_pairs={{0,1},{1,0},{2,3},{3,2},{4,5},{5,4},{6,7},{7,6},{8,9},{9,8},{10,11... | collective-permute-start | bytes 786440 | tf_op jit(solution)/shard_map/ppermute | solution.py:445
  71.0 23.1 %collective-permute-start.30 = (bf16[128,1024]{1,0:T(8,128)(2,1)S(1)}, bf16[128,1024]{1,0:T(8,128)(2,1)S(1)}, u32[]{:S(2)}, u32[]{:S(2)}) collective-permute-start(bf16[128,1024]{1,0:T(8,128)(2,1)S(1)} %copy-done.4), channel_id=1, source_target_pairs={{0,1},{1,0},{2,3},{3,2},{4,5},{5,4},{6,7},{7,6},{8,9},{9,8},{10,11... | collective-permute-start | bytes 786440 | tf_op jit(solution)/shard_map/ppermute | solution.py:445
  71.5 20.6 %collective-permute-start.27 = (bf16[128,1024]{1,0:T(8,128)(2,1)S(1)}, bf16[128,1024]{1,0:T(8,128)(2,1)S(1)}, u32[]{:S(2)}, u32[]{:S(2)}) collective-permute-start(bf16[128,1024]{1,0:T(8,128)(2,1)S(1)} %copy-done.4), channel_id=1, source_target_pairs={{0,2},{1,3},{2,0},{3,1},{4,6},{5,7},{6,4},{7,5},{8,10},{9,11},{10,... | collective-permute-start | bytes 786440 | tf_op jit(solution)/shard_map/ppermute | solution.py:445
  77.5 16.6 %collective-permute-start.33 = (bf16[128,1024]{1,0:T(8,128)(2,1)S(1)}, bf16[128,1024]{1,0:T(8,128)(2,1)S(1)}, u32[]{:S(2)}, u32[]{:S(2)}) collective-permute-start(bf16[128,1024]{1,0:T(8,128)(2,1)S(1)} %collective-permute-done.29.refs_3_), channel_id=1, source_target_pairs={{0,1},{1,0},{2,3},{3,2},{4,5},{5,4},{6,7},{7,6},{8,9},{9,8},{10,11... | collective-permute-start | bytes 786440 | tf_op jit(solution)/shard_map/ppermute | solution.py:445
  82.6 11.6 %collective-permute-start.32 = (bf16[128,1024]{1,0:T(8,128)(2,1)S(1)}, bf16[128,1024]{1,0:T(8,128)(2,1)S(1)}, u32[]{:S(2)}, u32[]{:S(2)}) collective-permute-start(bf16[128,1024]{1,0:T(8,128)(2,1)S(1)} %collective-permute-done.28.refs_2_), channel_id=1, source_target_pairs={{0,1},{1,0},{2,3},{3,2},{4,5},{5,4},{6,7},{7,6},{8,9},{9,8},{10,11... | collective-permute-start | bytes 786440 | tf_op jit(solution)/shard_map/ppermute | solution.py:445
  113.4 9.2 %collective-permute-start.35 = (bf16[128,1024]{1,0:T(8,128)(2,1)S(1)}, bf16[128,1024]{1,0:T(8,128)(2,1)S(1)}, u32[]{:S(2)}, u32[]{:S(2)}) collective-permute-start(bf16[128,1024]{1,0:T(8,128)(2,1)S(1)} %get-tuple-element.108), channel_id=1, source_target_pairs={{0,2},{1,3},{2,0},{3,1},{4,6},{5,7},{6,4},{7,5},{8,10},{9,11},{10,... | collective-permute-start | bytes 786440 | tf_op jit(solution)/shard_map/ppermute | solution.py:445
  114.7 13.8 %collective-permute-start.37 = (bf16[128,1024]{1,0:T(8,128)(2,1)S(1)}, bf16[128,1024]{1,0:T(8,128)(2,1)S(1)}, u32[]{:S(2)}, u32[]{:S(2)}) collective-permute-start(bf16[128,1024]{1,0:T(8,128)(2,1)S(1)} %get-tuple-element.109), channel_id=1, source_target_pairs={{0,6},{1,7},{2,4},{3,5},{4,2},{5,3},{6,0},{7,1},{8,14},{9,15},{10,... | collective-permute-start | bytes 786440 | tf_op jit(solution)/shard_map/ppermute | solution.py:445
  116.2 13.6 %collective-permute-start.36 = (bf16[128,1024]{1,0:T(8,128)(2,1)S(1)}, bf16[128,1024]{1,0:T(8,128)(2,1)S(1)}, u32[]{:S(2)}, u32[]{:S(2)}) collective-permute-start(bf16[128,1024]{1,0:T(8,128)(2,1)S(1)} %get-tuple-element.110), channel_id=1, source_target_pairs={{0,4},{1,5},{2,6},{3,7},{4,0},{5,1},{6,2},{7,3},{8,12},{9,13},{10,... | collective-permute-start | bytes 786440 | tf_op jit(solution)/shard_map/ppermute | solution.py:445
  118.0 27.7 %collective-permute-start.23 = (bf16[512,1024]{1,0:T(8,128)(2,1)S(1)}, bf16[512,1024]{1,0:T(8,128)(2,1)S(1)}, u32[]{:S(2)}, u32[]{:S(2)}) collective-permute-start(bf16[512,1024]{1,0:T(8,128)(2,1)S(1)} %convolution_convert_fusion.4), channel_id=1, source_target_pairs={{0,1},{1,0},{2,3},{3,2},{4,5},{5,4},{6,7},{7,6},{8,9},{9,8},{10,11... | collective-permute-start | bytes 3145736 | tf_op jit(solution)/shard_map/ppermute | solution.py:445
  131.4 10.2 %collective-permute-start.40 = (bf16[128,1024]{1,0:T(8,128)(2,1)S(1)}, bf16[128,1024]{1,0:T(8,128)(2,1)S(1)}, u32[]{:S(2)}, u32[]{:S(2)}) collective-permute-start(bf16[128,1024]{1,0:T(8,128)(2,1)S(1)} %fusion.63.refs_0_), channel_id=1, source_target_pairs={{0,6},{1,7},{2,4},{3,5},{4,2},{5,3},{6,0},{7,1},{8,14},{9,15},{10,... | collective-permute-start | bytes 786440 | tf_op jit(solution)/shard_map/ppermute | solution.py:445
  132.8 12.4 %collective-permute-start.39 = (bf16[128,1024]{1,0:T(8,128)(2,1)S(1)}, bf16[128,1024]{1,0:T(8,128)(2,1)S(1)}, u32[]{:S(2)}, u32[]{:S(2)}) collective-permute-start(bf16[128,1024]{1,0:T(8,128)(2,1)S(1)} %fusion.63.refs_0_), channel_id=1, source_target_pairs={{0,4},{1,5},{2,6},{3,7},{4,0},{5,1},{6,2},{7,3},{8,12},{9,13},{10,... | collective-permute-start | bytes 786440 | tf_op jit(solution)/shard_map/ppermute | solution.py:445
  133.9 11.4 %collective-permute-start.38 = (bf16[128,1024]{1,0:T(8,128)(2,1)S(1)}, bf16[128,1024]{1,0:T(8,128)(2,1)S(1)}, u32[]{:S(2)}, u32[]{:S(2)}) collective-permute-start(bf16[128,1024]{1,0:T(8,128)(2,1)S(1)} %fusion.63.refs_0_), channel_id=1, source_target_pairs={{0,2},{1,3},{2,0},{3,1},{4,6},{5,7},{6,4},{7,5},{8,10},{9,11},{10,... | collective-permute-start | bytes 786440 | tf_op jit(solution)/shard_map/ppermute | solution.py:445
  136.1 11.9 %collective-permute-start.41 = (bf16[128,1024]{1,0:T(8,128)(2,1)S(1)}, bf16[128,1024]{1,0:T(8,128)(2,1)S(1)}, u32[]{:S(2)}, u32[]{:S(2)}) collective-permute-start(bf16[128,1024]{1,0:T(8,128)(2,1)S(1)} %fusion.63.refs_0_), channel_id=1, source_target_pairs={{0,1},{1,0},{2,3},{3,2},{4,5},{5,4},{6,7},{7,6},{8,9},{9,8},{10,11... | collective-permute-start | bytes 786440 | tf_op jit(solution)/shard_map/ppermute | solution.py:445
  141.6 7.6 %collective-permute-start.44 = (bf16[128,1024]{1,0:T(8,128)(2,1)S(1)}, bf16[128,1024]{1,0:T(8,128)(2,1)S(1)}, u32[]{:S(2)}, u32[]{:S(2)}) collective-permute-start(bf16[128,1024]{1,0:T(8,128)(2,1)S(1)} %collective-permute-done.40.refs_3_), channel_id=1, source_target_pairs={{0,1},{1,0},{2,3},{3,2},{4,5},{5,4},{6,7},{7,6},{8,9},{9,8},{10,11... | collective-permute-start | bytes 786440 | tf_op jit(solution)/shard_map/ppermute | solution.py:445
  147.0 55.2 %collective-permute-start.24 = (bf16[128,1024]{1,0:T(8,128)(2,1)}, bf16[128,1024]{1,0:T(8,128)(2,1)}, u32[]{:S(2)}, u32[]{:S(2)}) collective-permute-start(bf16[128,1024]{1,0:T(8,128)(2,1)} %get-tuple-element.111), channel_id=1, source_target_pairs={{0,2},{1,3},{2,0},{3,1},{4,6},{5,7},{6,4},{7,5},{8,10},{9,11},{10,... | collective-permute-start | bytes 786440 | tf_op jit(solution)/shard_map/ppermute | solution.py:445
  148.0 54.1 %collective-permute-start.26 = (bf16[128,1024]{1,0:T(8,128)(2,1)}, bf16[128,1024]{1,0:T(8,128)(2,1)}, u32[]{:S(2)}, u32[]{:S(2)}) collective-permute-start(bf16[128,1024]{1,0:T(8,128)(2,1)} %get-tuple-element.112), channel_id=1, source_target_pairs={{0,6},{1,7},{2,4},{3,5},{4,2},{5,3},{6,0},{7,1},{8,14},{9,15},{10,... | collective-permute-start | bytes 786440 | tf_op jit(solution)/shard_map/ppermute | solution.py:445
  168.2 14.8 %collective-permute-start.45 = (bf16[512,1024]{1,0:T(8,128)(2,1)S(1)}, bf16[512,1024]{1,0:T(8,128)(2,1)S(1)}, u32[]{:S(2)}, u32[]{:S(2)}) collective-permute-start(bf16[512,1024]{1,0:T(8,128)(2,1)S(1)} %convolution_convert_fusion.3), channel_id=1, source_target_pairs={{0,1},{1,0},{2,3},{3,2},{4,5},{5,4},{6,7},{7,6},{8,9},{9,8},{10,11... | collective-permute-start | bytes 3145736 | tf_op jit(solution)/shard_map/ppermute | solution.py:445
  183.3 9.2 %collective-permute-start.46 = (bf16[128,1024]{1,0:T(8,128)(2,1)S(1)}, bf16[128,1024]{1,0:T(8,128)(2,1)S(1)}, u32[]{:S(2)}, u32[]{:S(2)}) collective-permute-start(bf16[128,1024]{1,0:T(8,128)(2,1)S(1)} %get-tuple-element.105), channel_id=1, source_target_pairs={{0,2},{1,3},{2,0},{3,1},{4,6},{5,7},{6,4},{7,5},{8,10},{9,11},{10,... | collective-permute-start | bytes 786440 | tf_op jit(solution)/shard_map/ppermute | solution.py:445
  184.6 13.5 %collective-permute-start.48 = (bf16[128,1024]{1,0:T(8,128)(2,1)S(1)}, bf16[128,1024]{1,0:T(8,128)(2,1)S(1)}, u32[]{:S(2)}, u32[]{:S(2)}) collective-permute-start(bf16[128,1024]{1,0:T(8,128)(2,1)S(1)} %get-tuple-element.106), channel_id=1, source_target_pairs={{0,6},{1,7},{2,4},{3,5},{4,2},{5,3},{6,0},{7,1},{8,14},{9,15},{10,... | collective-permute-start | bytes 786440 | tf_op jit(solution)/shard_map/ppermute | solution.py:445
  186.1 14.8 %collective-permute-start.47 = (bf16[128,1024]{1,0:T(8,128)(2,1)S(1)}, bf16[128,1024]{1,0:T(8,128)(2,1)S(1)}, u32[]{:S(2)}, u32[]{:S(2)}) collective-permute-start(bf16[128,1024]{1,0:T(8,128)(2,1)S(1)} %get-tuple-element.107), channel_id=1, source_target_pairs={{0,4},{1,5},{2,6},{3,7},{4,0},{5,1},{6,2},{7,3},{8,12},{9,13},{10,... | collective-permute-start | bytes 786440 | tf_op jit(solution)/shard_map/ppermute | solution.py:445
  192.5 12.7 %collective-permute-start.25 = (bf16[128,1024]{1,0:T(8,128)(2,1)}, bf16[128,1024]{1,0:T(8,128)(2,1)}, u32[]{:S(2)}, u32[]{:S(2)}) collective-permute-start(bf16[128,1024]{1,0:T(8,128)(2,1)} %get-tuple-element.113), channel_id=1, source_target_pairs={{0,4},{1,5},{2,6},{3,7},{4,0},{5,1},{6,2},{7,3},{8,12},{9,13},{10,... | collective-permute-start | bytes 786440 | tf_op jit(solution)/shard_map/ppermute | solution.py:445
  198.1 40.7 %collective-permute-start.61 = (bf16[64,3072]{1,0:T(8,128)(2,1)}, bf16[64,3072]{1,0:T(8,128)(2,1)}, u32[]{:S(2)}, u32[]{:S(2)}) collective-permute-start(bf16[64,3072]{1,0:T(8,128)(2,1)} %get-tuple-element.114), channel_id=1, source_target_pairs={{0,8},{8,0},{16,24},{24,16},{1,9},{9,1},{17,25},{25,17},{2,10},{10... | collective-permute-start | bytes 1179656 | tf_op jit(solution)/shard_map/ppermute | solution.py:449
  202.0 36.8 %collective-permute-start.49 = (f32[1,2176]{1,0:T(1,128)S(1)}, f32[1,2176]{1,0:T(1,128)S(1)}, u32[]{:S(2)}, u32[]{:S(2)}) collective-permute-start(f32[1,2176]{1,0:T(1,128)S(1)} %broadcast_in_dim.62), channel_id=1, source_target_pairs={{0,1},{1,0},{2,3},{3,2},{4,5},{5,4},{6,7},{7,6},{8,9},{9,8},{10,11... | collective-permute-start | bytes 26120 | tf_op jit(solution)/shard_map/ppermute | solution.py:445
  252.6 9.6 %collective-permute-start.62 = (bf16[32,3072]{1,0:T(8,128)(2,1)S(1)}, bf16[32,3072]{1,0:T(8,128)(2,1)S(1)}, u32[]{:S(2)}, u32[]{:S(2)}) collective-permute-start(bf16[32,3072]{1,0:T(8,128)(2,1)S(1)} %get-tuple-element.118), channel_id=1, source_target_pairs={{0,16},{8,24},{16,0},{24,8},{1,17},{9,25},{17,1},{25,9},{2,18},{10... | collective-permute-start | bytes 589832 | tf_op jit(solution)/shard_map/ppermute | solution.py:449
  262.2 10.2 %collective-permute-start.63 = (bf16[32,3072]{1,0:T(8,128)(2,1)S(1)}, bf16[32,3072]{1,0:T(8,128)(2,1)S(1)}, u32[]{:S(2)}, u32[]{:S(2)}) collective-permute-start(bf16[32,3072]{1,0:T(8,128)(2,1)S(1)} %add_convert_fusion.2), channel_id=1, source_target_pairs={{0,16},{8,24},{16,0},{24,8},{1,17},{9,25},{17,1},{25,9},{2,18},{10... | collective-permute-start | bytes 589832 | tf_op jit(solution)/shard_map/ppermute | solution.py:449
  272.5 11.1 %collective-permute-start.64 = (bf16[64,3072]{1,0:T(8,128)(2,1)S(1)}, bf16[64,3072]{1,0:T(8,128)(2,1)S(1)}, u32[]{:S(2)}, u32[]{:S(2)}) collective-permute-start(bf16[64,3072]{1,0:T(8,128)(2,1)S(1)} %maximum_select_fusion.1), channel_id=1, source_target_pairs={{0,8},{8,0},{16,24},{24,16},{1,9},{9,1},{17,25},{25,17},{2,10},{10... | collective-permute-start | bytes 1179656 | tf_op jit(solution)/shard_map/ppermute | solution.py:449
  (75 other events, 900.3 us)
Sparse Core Ops, SparseCore 0:
  108.4 141.3 all-reduce.1
where the time goes:
time: 294 us
  waiting for transfers between devices  137 us (47%)
  starting transfers between devices  50.7 us (17%)
  Pallas kernels  38.3 us (13%)
  matrix products  21 us (7%)
  other arithmetic  19.3 us (7%)
  between operations  15 us (5%)
  local copies, waits for them, and re-layouts  12.8 us (4%)
    ppermute x59, waiting for transfers between devices, group_swap(): lax.ppermute(values, group_axes, [(rank, rank ^ mask) for rank in range(8)])  79.3 us
    ppermute x6, waiting for transfers between devices, rep_swap(): lax.ppermute(values, 'rep', [(rank, rank ^ mask) for rank in range(4)])  57.4 us
    ppermute x59, starting transfers between devices, group_swap(): lax.ppermute(values, group_axes, [(rank, rank ^ mask) for rank in range(8)])  45.8 us
    pallas_call x1, Pallas kernels, call(): pl.pallas_call(kernel, name='attention_backward', in_specs=[scalar_spec()...  15.1 us
    dot_general x6, matrix products, dot_plain(): return jnp.dot(left, right, preferred_element_type=jnp.float32)  10.2 us
    pallas_call x1, Pallas kernels, call(): pl.pallas_call(kernel, name='attention_forward', in_specs=[scalar_spec(),...  10.2 us
    pallas_call x1, Pallas kernels, residual_stage(): pl.pallas_call(kernel, name='residual_stage', in_specs=[scalar_spec(), wh...  8.03 us
    dot_general x5, matrix products, dot_last(): lax.dot_general(left, right, contract_last, preferred_element_type=jnp.fl...  6.12 us
  transfers between devices with their start and end apart: 66, of which 28 were waited for; matrix products, arithmetic and copies ran while one was open for 12% of the time, Pallas kernels for 12%

commit v1 on v0

--- a/solution.py
+++ b/solution.py
@@ -1123,7 +1123,10 @@
     )
     mix_near = gather_near(mix)
     mix_far = gather_far(mix_near)
-    grad_near = gather_near(after(out_grad, mix_near[1:]))
+    grad_own = after(out_grad, mix_near[1:])
+    grad_near = [grad_own]
+    for mask in (2, 4, 6):
+        grad_near.append(group_swap(grad_own, mask))
     grad_all = stack_rows(grad_near + gather_far(grad_near))
 
     normed_mid, mix_all, out_cols, own_resid, own_hat, own_scale = residual_stage(

time: 294 us -> 294 us (level)
  no operation moved by 1% of the time
where the time goes in v1:
time: 294 us
  waiting for transfers between devices  137 us (47%)
  starting transfers between devices  50.7 us (17%)
  Pallas kernels  38.3 us (13%)
  matrix products  21 us (7%)
  other arithmetic  19.3 us (7%)
  between operations  15 us (5%)
  local copies, waits for them, and re-layouts  12.8 us (4%)
    ppermute x59, waiting for transfers between devices, group_swap(): lax.ppermute(values, group_axes, [(rank, rank ^ mask) for rank in range(8)])  79.3 us
    ppermute x6, waiting for transfers between devices, rep_swap(): lax.ppermute(values, 'rep', [(rank, rank ^ mask) for rank in range(4)])  57.4 us
    ppermute x59, starting transfers between devices, group_swap(): lax.ppermute(values, group_axes, [(rank, rank ^ mask) for rank in range(8)])  45.8 us
    pallas_call x1, Pallas kernels, call(): pl.pallas_call(kernel, name='attention_backward', in_specs=[scalar_spec()...  15.1 us
    dot_general x6, matrix products, dot_plain(): return jnp.dot(left, right, preferred_element_type=jnp.float32)  10.2 us
    pallas_call x1, Pallas kernels, call(): pl.pallas_call(kernel, name='attention_forward', in_specs=[scalar_spec(),...  10.2 us
    pallas_call x1, Pallas kernels, residual_stage(): pl.pallas_call(kernel, name='residual_stage', in_specs=[scalar_spec(), wh...  8.03 us
    dot_general x5, matrix products, dot_last(): lax.dot_general(left, right, contract_last, preferred_element_type=jnp.fl...  6.12 us
  transfers between devices with their start and end apart: 66, of which 28 were waited for; matrix products, arithmetic and copies ran while one was open for 12% of the time, Pallas kernels for 12%

profile of v1, /device:TPU:0, one launch (start us, length us, event | category | flops | bytes accessed | tf_op | source)
XLA Modules:
  0.0 293.9 jit_solution(16836039829711606112)
XLA Ops:
  7.8 3.5 %collective-permute-start.5 = (bf16[128,1024]{1,0:T(8,128)(2,1)}, bf16[128,1024]{1,0:T(8,128)(2,1)S(1)}, u32[]{:S(2)}, u32[]{:S(2)}) collective-permute-start(bf16[128,1024]{1,0:T(8,128)(2,1)} %refs_16_.1), channel_id=1, source_target_pairs={{0,6},{1,7},{2,4},{3,5},{4,2},{5,3},{6,0},{7,1},{8,14},{9,15},{10,... | collective-permute-start | bytes 786440 | tf_op jit(solution)/shard_map/ppermute | solution.py:445
  12.6 2.2 pack_heads.1
  14.8 1.9 collective-permute-start
  18.4 8.9 %collective-permute-done.piece_1 = bf16[256,256]{1,0:T(8,128)(2,1)} collective-permute-done((bf16[256,256]{1,0:T(8,128)(2,1)}, bf16[256,256]{1,0:T(8,128)(2,1)}, u32[]{:S(2)}, u32[]{:S(2)}) %collective-permute-start) | collective-permute-done | bytes 131104 | tf_op jit(solution)/shard_map/ppermute | solution.py:445
  28.2 3.0 %fusion.31 = (f32[1024,128]{1,0:T(8,128)}, f32[1024,128]{1,0:T(8,128)}) fusion(s32[128]{0:T(128)S(1)} %get-tuple-element.126, s32[128]{0:T(128)S(1)} %get-tuple-element.127, f32[128]{0:T(128)S(1)} %mul.140, f32[1024]{0:T(1024)S(1)} %subtract_convert_fusion, pred[128]{0:T(512)(128)(4,1)S(1)} %compare_and_fusion), kind=kLoop, calls=%fused_computation.50 | loop fusion | flops 655360 | bytes 1054336 | tf_op jit(solution)/shard_map/mul | solution.py:1114
  35.7 1.8 constant_dynamic-slice_fusion.4
  37.4 1.9 collective-permute-done.2.piece_3
  39.3 2.3 collective-permute-start.19
  42.9 10.2 %attention_forward.1 = (bf16[1024,128]{1,0:T(8,128)(2,1)S(1)}, bf16[1024,1024]{1,0:T(8,128)(2,1)}, f32[1024,256]{1,0:T(8,128)}, f32[2048,1]{1,0:T(8,128)}, bf16[1024,256]{1,0:T(8,128)(2,1)}) custom-call(s32[2]{0:T(128)S(1)} %copy-done.13, f32[1,1024]{1,0:T(1,128)S(1)} %bitcast.40, bf16[256,256]{1,0:T(8,128)(2,1)} %get-tuple-element.52.piece_0, ...), custom_call_target="tpu_custom_call" | custom-call | tf_op jit(solution)/shard_map/attention_forward/pallas_call | solution.py:720
  53.1 2.4 collective-permute-start.12
  57.2 6.2 %collective-permute-done.12.refs_3_ = bf16[1024,128]{1,0:T(8,128)(2,1)} collective-permute-done((bf16[1024,128]{1,0:T(8,128)(2,1)S(1)}, bf16[1024,128]{1,0:T(8,128)(2,1)}, u32[]{:S(2)}, u32[]{:S(2)}) %collective-permute-start.12) | collective-permute-done | bytes 262176 | tf_op jit(solution)/shard_map/ppermute | solution.py:445
  63.4 3.3 %collective-permute-done.11.refs_2_ = bf16[1024,128]{1,0:T(8,128)(2,1)} collective-permute-done((bf16[1024,128]{1,0:T(8,128)(2,1)S(1)}, bf16[1024,128]{1,0:T(8,128)(2,1)}, u32[]{:S(2)}, u32[]{:S(2)}) %collective-permute-start.11) | collective-permute-done | bytes 262176 | tf_op jit(solution)/shard_map/ppermute | solution.py:445
  67.3 1.8 collective-permute-start.29
  72.2 5.3 %collective-permute-done.29.refs_3_ = bf16[128,1024]{1,0:T(8,128)(2,1)S(1)} collective-permute-done((bf16[128,1024]{1,0:T(8,128)(2,1)S(1)}, bf16[128,1024]{1,0:T(8,128)(2,1)S(1)}, u32[]{:S(2)}, u32[]{:S(2)}) %collective-permute-start.29) | collective-permute-done | bytes 262176 | tf_op jit(solution)/shard_map/ppermute | solution.py:445
  77.5 5.0 %collective-permute-done.28.refs_2_ = bf16[128,1024]{1,0:T(8,128)(2,1)S(1)} collective-permute-done((bf16[128,1024]{1,0:T(8,128)(2,1)S(1)}, bf16[128,1024]{1,0:T(8,128)(2,1)S(1)}, u32[]{:S(2)}, u32[]{:S(2)}) %collective-permute-start.28) | collective-permute-done | bytes 262176 | tf_op jit(solution)/shard_map/ppermute | solution.py:445
  82.6 8.0 %residual_stage.1 = (bf16[1024,1024]{1,0:T(8,128)(2,1)S(1)}, bf16[1024,1024]{1,0:T(8,128)(2,1)}, bf16[1024,128]{1,0:T(8,128)(2,1)}, f32[128,1024]{1,0:T(8,128)},...) custom-call(s32[2]{0:T(128)S(1)} %copy-done.13, f32[1,1024]{1,0:T(1,128)S(1)} %bitcast.39, bf16[1024,128]{1,0:T(8,128)(2,1)} %copy-done.6, ...), custom_call_target="tpu_custom_call" | custom-call | tf_op jit(solution)/shard_map/residual_stage/pallas_call | solution.py:811
  94.6 2.3 multiply_convert_fusion
  101.2 2.0 pad_maximum_fusion
  103.2 2.6 fusion.10
  105.8 2.0 add_convert_fusion
  108.3 2.6 fusion.12
  114.7 1.5 collective-permute-start.37
  118.1 4.6 %collective-permute-done.35 = bf16[128,1024]{1,0:T(8,128)(2,1)S(1)} collective-permute-done((bf16[128,1024]{1,0:T(8,128)(2,1)S(1)}, bf16[128,1024]{1,0:T(8,128)(2,1)S(1)}, u32[]{:S(2)}, u32[]{:S(2)}) %collective-permute-start.35) | collective-permute-done | bytes 262176 | tf_op jit(solution)/shard_map/ppermute | solution.py:445
  122.7 5.8 %collective-permute-done.37 = bf16[128,1024]{1,0:T(8,128)(2,1)S(1)} collective-permute-done((bf16[128,1024]{1,0:T(8,128)(2,1)S(1)}, bf16[128,1024]{1,0:T(8,128)(2,1)S(1)}, u32[]{:S(2)}, u32[]{:S(2)}) %collective-permute-start.37) | collective-permute-done | bytes 262176 | tf_op jit(solution)/shard_map/ppermute | solution.py:445
  136.1 5.4 %collective-permute-done.40.refs_3_ = bf16[128,1024]{1,0:T(8,128)(2,1)S(1)} collective-permute-done((bf16[128,1024]{1,0:T(8,128)(2,1)S(1)}, bf16[128,1024]{1,0:T(8,128)(2,1)S(1)}, u32[]{:S(2)}, u32[]{:S(2)}) %collective-permute-start.40) | collective-permute-done | bytes 262176 | tf_op jit(solution)/shard_map/ppermute | solution.py:445
  141.6 3.7 %collective-permute-done.39.refs_2_ = bf16[128,1024]{1,0:T(8,128)(2,1)S(1)} collective-permute-done((bf16[128,1024]{1,0:T(8,128)(2,1)S(1)}, bf16[128,1024]{1,0:T(8,128)(2,1)S(1)}, u32[]{:S(2)}, u32[]{:S(2)}) %collective-permute-start.39) | collective-permute-done | bytes 262176 | tf_op jit(solution)/shard_map/ppermute | solution.py:445
  150.1 15.1 %attention_backward.1 = (bf16[1024,256]{1,0:T(8,128)(2,1)S(1)}, f32[1,128]{1,0:T(1,128)S(1)}, f32[1,128]{1,0:T(1,128)S(1)}, bf16[1024,128]{1,0:T(8,128)(2,1)S(1)...) custom-call(s32[2]{0:T(128)S(1)} %copy-done.13, ...), custom_call_target="tpu_custom_call" | custom-call | tf_op jit(solution)/shard_map/attention_backward/pallas_call | solution.py:1004
  168.6 2.4 collective-permute-done.55
  173.3 2.0 collective-permute-done.57
  175.3 2.3 collective-permute-start.59
  178.2 2.3 collective-permute-done.59
  180.5 2.0 collective-permute-done.60
  184.6 1.5 collective-permute-start.48
  187.8 4.8 %collective-permute-done.46 = bf16[128,1024]{1,0:T(8,128)(2,1)S(1)} collective-permute-done((bf16[128,1024]{1,0:T(8,128)(2,1)S(1)}, bf16[128,1024]{1,0:T(8,128)(2,1)S(1)}, u32[]{:S(2)}, u32[]{:S(2)}) %collective-permute-start.46) | collective-permute-done | bytes 262176 | tf_op jit(solution)/shard_map/ppermute | solution.py:445
  193.8 4.3 %collective-permute-done.48 = bf16[128,1024]{1,0:T(8,128)(2,1)S(1)} collective-permute-done((bf16[128,1024]{1,0:T(8,128)(2,1)S(1)}, bf16[128,1024]{1,0:T(8,128)(2,1)S(1)}, u32[]{:S(2)}, u32[]{:S(2)}) %collective-permute-start.48) | collective-permute-done | bytes 262176 | tf_op jit(solution)/shard_map/ppermute | solution.py:445
  198.1 1.7 collective-permute-start.61
  202.1 3.1 %collective-permute-done.25 = bf16[128,1024]{1,0:T(8,128)(2,1)} collective-permute-done((bf16[128,1024]{1,0:T(8,128)(2,1)}, bf16[128,1024]{1,0:T(8,128)(2,1)}, u32[]{:S(2)}, u32[]{:S(2)}) %collective-permute-start.25) | collective-permute-done | bytes 262176 | tf_op jit(solution)/shard_map/ppermute | solution.py:445
  205.2 2.6 fusion.50
  207.8 31.0 %collective-permute-done.61 = bf16[64,3072]{1,0:T(8,128)(2,1)} collective-permute-done((bf16[64,3072]{1,0:T(8,128)(2,1)}, bf16[64,3072]{1,0:T(8,128)(2,1)}, u32[]{:S(2)}, u32[]{:S(2)}) %collective-permute-start.61) | collective-permute-done | bytes 393248 | tf_op jit(solution)/shard_map/ppermute | solution.py:449
  240.9 1.6 collective-permute-done.50
  243.3 3.0 %collective-permute-done.51 = f32[1,2176]{1,0:T(1,128)S(1)} collective-permute-done((f32[1,2176]{1,0:T(1,128)S(1)}, f32[1,2176]{1,0:T(1,128)S(1)}, u32[]{:S(2)}, u32[]{:S(2)}) %collective-permute-start.51) | collective-permute-done | bytes 8736 | tf_op jit(solution)/shard_map/ppermute | solution.py:445
  246.4 3.6 %collective-permute-done.52 = f32[1,2176]{1,0:T(1,128)S(1)} collective-permute-done((f32[1,2176]{1,0:T(1,128)S(1)}, f32[1,2176]{1,0:T(1,128)S(1)}, u32[]{:S(2)}, u32[]{:S(2)}) %collective-permute-start.52) | collective-permute-done | bytes 8736 | tf_op jit(solution)/shard_map/ppermute | solution.py:449
  252.6 1.6 collective-permute-start.62
  255.4 6.8 %collective-permute-done.62 = bf16[32,3072]{1,0:T(8,128)(2,1)S(1)} collective-permute-done((bf16[32,3072]{1,0:T(8,128)(2,1)S(1)}, bf16[32,3072]{1,0:T(8,128)(2,1)S(1)}, u32[]{:S(2)}, u32[]{:S(2)}) %collective-permute-start.62) | collective-permute-done | bytes 196640 | tf_op jit(solution)/shard_map/ppermute | solution.py:449
  262.9 9.5 %collective-permute-done.63 = bf16[32,3072]{1,0:T(8,128)(2,1)S(1)} collective-permute-done((bf16[32,3072]{1,0:T(8,128)(2,1)S(1)}, bf16[32,3072]{1,0:T(8,128)(2,1)S(1)}, u32[]{:S(2)}, u32[]{:S(2)}) %collective-permute-start.63) | collective-permute-done | bytes 196640 | tf_op jit(solution)/shard_map/ppermute | solution.py:449
  272.6 5.2 %fusion.66 = (f32[576,1024]{1,0:T(8,128)}, f32[576,1024]{1,0:T(8,128)}, f32[576,1024]{1,0:T(8,128)}) fusion(bf16[1728,1024]{1,0:T(8,128)(2,1)} %all-reduce.2.cloned.1.call-done), kind=kLoop, calls=%fused_computation.133 | loop fusion | bytes 14155776 | tf_op jit(solution)/shard_map/slice | solution.py:1221
  277.8 5.8 %collective-permute-done.64 = bf16[64,3072]{1,0:T(8,128)(2,1)S(1)} collective-permute-done((bf16[64,3072]{1,0:T(8,128)(2,1)S(1)}, bf16[64,3072]{1,0:T(8,128)(2,1)S(1)}, u32[]{:S(2)}, u32[]{:S(2)}) %collective-permute-start.64) | collective-permute-done | bytes 393248 | tf_op jit(solution)/shard_map/ppermute | solution.py:449
  284.6 2.4 unpack_heads.1
  (273 shorter events, 64.0 us)
Async XLA Ops:
  7.2 265.4 %all-reduce.2.cloned.1.call-start = ((), (), s32[]{:S(2)}) async-start(), calls=%async_computation | async-start | bytes 7077888 | tf_op jit(solution)/shard_map/psum | solution.py:1164
  7.3 34.3 %collective-permute-start.6 = (bf16[128,1024]{1,0:T(8,128)(2,1)}, bf16[128,1024]{1,0:T(8,128)(2,1)S(1)}, u32[]{:S(2)}, u32[]{:S(2)}) collective-permute-start(bf16[128,1024]{1,0:T(8,128)(2,1)} %refs_16_.1), channel_id=1, source_target_pairs={{0,1},{1,0},{2,3},{3,2},{4,5},{5,4},{6,7},{7,6},{8,9},{9,8},{10,11... | collective-permute-start | bytes 786440 | tf_op jit(solution)/shard_map/ppermute | solution.py:445
  7.8 19.8 %collective-permute-start.5 = (bf16[128,1024]{1,0:T(8,128)(2,1)}, bf16[128,1024]{1,0:T(8,128)(2,1)S(1)}, u32[]{:S(2)}, u32[]{:S(2)}) collective-permute-start(bf16[128,1024]{1,0:T(8,128)(2,1)} %refs_16_.1), channel_id=1, source_target_pairs={{0,6},{1,7},{2,4},{3,5},{4,2},{5,3},{6,0},{7,1},{8,14},{9,15},{10,... | collective-permute-start | bytes 786440 | tf_op jit(solution)/shard_map/ppermute | solution.py:445
  11.3 16.3 %collective-permute-start.4 = (bf16[128,1024]{1,0:T(8,128)(2,1)}, bf16[128,1024]{1,0:T(8,128)(2,1)S(1)}, u32[]{:S(2)}, u32[]{:S(2)}) collective-permute-start(bf16[128,1024]{1,0:T(8,128)(2,1)} %refs_16_.1), channel_id=1, source_target_pairs={{0,4},{1,5},{2,6},{3,7},{4,0},{5,1},{6,2},{7,3},{8,12},{9,13},{10,... | collective-permute-start | bytes 786440 | tf_op jit(solution)/shard_map/ppermute | solution.py:445
  11.8 16.3 %collective-permute-start.3 = (bf16[128,1024]{1,0:T(8,128)(2,1)}, bf16[128,1024]{1,0:T(8,128)(2,1)S(1)}, u32[]{:S(2)}, u32[]{:S(2)}) collective-permute-start(bf16[128,1024]{1,0:T(8,128)(2,1)} %refs_16_.1), channel_id=1, source_target_pairs={{0,2},{1,3},{2,0},{3,1},{4,6},{5,7},{6,4},{7,5},{8,10},{9,11},{10,... | collective-permute-start | bytes 786440 | tf_op jit(solution)/shard_map/ppermute | solution.py:445
  14.8 12.5 %collective-permute-start = (bf16[256,256]{1,0:T(8,128)(2,1)}, bf16[256,256]{1,0:T(8,128)(2,1)}, u32[]{:S(2)}, u32[]{:S(2)}) collective-permute-start(bf16[256,256]{1,0:T(8,128)(2,1)} %get-tuple-element.53), channel_id=1, source_target_pairs={{0,2},{1,3},{2,0},{3,1},{4,6},{5,7},{6,4},{7,5},{8,10},{9,11},{10,... | collective-permute-start | bytes 393224 | tf_op jit(solution)/shard_map/ppermute | solution.py:445
  27.3 5.2 %collective-permute-start.1 = (bf16[256,256]{1,0:T(8,128)(2,1)}, bf16[256,256]{1,0:T(8,128)(2,1)S(1)}, u32[]{:S(2)}, u32[]{:S(2)}) collective-permute-start(bf16[256,256]{1,0:T(8,128)(2,1)} %get-tuple-element.54), channel_id=1, source_target_pairs={{0,4},{1,5},{2,6},{3,7},{4,0},{5,1},{6,2},{7,3},{8,12},{9,13},{10,... | collective-permute-start | bytes 393224 | tf_op jit(solution)/shard_map/ppermute | solution.py:445
  27.6 14.7 %collective-permute-start.9 = (bf16[128,1024]{1,0:T(8,128)(2,1)S(1)}, bf16[128,1024]{1,0:T(8,128)(2,1)}, u32[]{:S(2)}, u32[]{:S(2)}) collective-permute-start(bf16[128,1024]{1,0:T(8,128)(2,1)S(1)} %collective-permute-done.5.refs_3_.refs_19_), channel_id=1, source_target_pairs={{0,1},{1,0},{2,3},{3,2},{4,5},{5,4},{6,7},{7,6},{8,9},{9,8},{10,11... | collective-permute-start | bytes 786440 | tf_op jit(solution)/shard_map/ppermute | solution.py:445
  27.6 15.2 %collective-permute-start.8 = (bf16[128,1024]{1,0:T(8,128)(2,1)S(1)}, bf16[128,1024]{1,0:T(8,128)(2,1)}, u32[]{:S(2)}, u32[]{:S(2)}) collective-permute-start(bf16[128,1024]{1,0:T(8,128)(2,1)S(1)} %collective-permute-done.4.refs_2_.refs_18_), channel_id=1, source_target_pairs={{0,1},{1,0},{2,3},{3,2},{4,5},{5,4},{6,7},{7,6},{8,9},{9,8},{10,11... | collective-permute-start | bytes 786440 | tf_op jit(solution)/shard_map/ppermute | solution.py:445
  28.1 14.7 %collective-permute-start.7 = (bf16[128,1024]{1,0:T(8,128)(2,1)S(1)}, bf16[128,1024]{1,0:T(8,128)(2,1)}, u32[]{:S(2)}, u32[]{:S(2)}) collective-permute-start(bf16[128,1024]{1,0:T(8,128)(2,1)S(1)} %collective-permute-done.3.refs_1_.refs_17_), channel_id=1, source_target_pairs={{0,1},{1,0},{2,3},{3,2},{4,5},{5,4},{6,7},{7,6},{8,9},{9,8},{10,11... | collective-permute-start | bytes 786440 | tf_op jit(solution)/shard_map/ppermute | solution.py:445
  33.1 6.2 %collective-permute-start.2 = (bf16[256,256]{1,0:T(8,128)(2,1)}, bf16[256,256]{1,0:T(8,128)(2,1)}, u32[]{:S(2)}, u32[]{:S(2)}) collective-permute-start(bf16[256,256]{1,0:T(8,128)(2,1)} %get-tuple-element.55), channel_id=1, source_target_pairs={{0,6},{1,7},{2,4},{3,5},{4,2},{5,3},{6,0},{7,1},{8,14},{9,15},{10,... | collective-permute-start | bytes 393224 | tf_op jit(solution)/shard_map/ppermute | solution.py:445
  39.3 16.8 %collective-permute-start.19 = (bf16[128,1024]{1,0:T(8,128)(2,1)S(1)}, bf16[128,1024]{1,0:T(8,128)(2,1)S(1)}, u32[]{:S(2)}, u32[]{:S(2)}) collective-permute-start(bf16[128,1024]{1,0:T(8,128)(2,1)S(1)} %get-tuple-element.57.refs_8_), channel_id=1, source_target_pairs={{0,6},{1,7},{2,4},{3,5},{4,2},{5,3},{6,0},{7,1},{8,14},{9,15},{10,... | collective-permute-start | bytes 786440 | tf_op jit(solution)/shard_map/ppermute | solution.py:445
  41.6 15.1 %collective-permute-start.18 = (bf16[128,1024]{1,0:T(8,128)(2,1)S(1)}, bf16[128,1024]{1,0:T(8,128)(2,1)S(1)}, u32[]{:S(2)}, u32[]{:S(2)}) collective-permute-start(bf16[128,1024]{1,0:T(8,128)(2,1)S(1)} %get-tuple-element.57.refs_8_), channel_id=1, source_target_pairs={{0,4},{1,5},{2,6},{3,7},{4,0},{5,1},{6,2},{7,3},{8,12},{9,13},{10,... | collective-permute-start | bytes 786440 | tf_op jit(solution)/shard_map/ppermute | solution.py:445
  42.3 14.4 %collective-permute-start.17 = (bf16[128,1024]{1,0:T(8,128)(2,1)S(1)}, bf16[128,1024]{1,0:T(8,128)(2,1)S(1)}, u32[]{:S(2)}, u32[]{:S(2)}) collective-permute-start(bf16[128,1024]{1,0:T(8,128)(2,1)S(1)} %get-tuple-element.57.refs_8_), channel_id=1, source_target_pairs={{0,2},{1,3},{2,0},{3,1},{4,6},{5,7},{6,4},{7,5},{8,10},{9,11},{10,... | collective-permute-start | bytes 786440 | tf_op jit(solution)/shard_map/ppermute | solution.py:445
  53.1 10.3 %collective-permute-start.12 = (bf16[1024,128]{1,0:T(8,128)(2,1)S(1)}, bf16[1024,128]{1,0:T(8,128)(2,1)}, u32[]{:S(2)}, u32[]{:S(2)}) collective-permute-start(bf16[1024,128]{1,0:T(8,128)(2,1)S(1)} %get-tuple-element.56.refs_0_.mix_ref), channel_id=1, source_target_pairs={{0,6},{1,7},{2,4},{3,5},{4,2},{5,3},{6,0},{7,1},{8,14},{9,15},{10,... | collective-permute-start | bytes 786440 | tf_op jit(solution)/shard_map/ppermute | solution.py:445
  55.5 11.2 %collective-permute-start.11 = (bf16[1024,128]{1,0:T(8,128)(2,1)S(1)}, bf16[1024,128]{1,0:T(8,128)(2,1)}, u32[]{:S(2)}, u32[]{:S(2)}) collective-permute-start(bf16[1024,128]{1,0:T(8,128)(2,1)S(1)} %get-tuple-element.56.refs_0_.mix_ref), channel_id=1, source_target_pairs={{0,4},{1,5},{2,6},{3,7},{4,0},{5,1},{6,2},{7,3},{8,12},{9,13},{10,... | collective-permute-start | bytes 786440 | tf_op jit(solution)/shard_map/ppermute | solution.py:445
  56.1 10.6 %collective-permute-start.10 = (bf16[1024,128]{1,0:T(8,128)(2,1)S(1)}, bf16[1024,128]{1,0:T(8,128)(2,1)}, u32[]{:S(2)}, u32[]{:S(2)}) collective-permute-start(bf16[1024,128]{1,0:T(8,128)(2,1)S(1)} %get-tuple-element.56.refs_0_.mix_ref), channel_id=1, source_target_pairs={{0,2},{1,3},{2,0},{3,1},{4,6},{5,7},{6,4},{7,5},{8,10},{9,11},{10,... | collective-permute-start | bytes 786440 | tf_op jit(solution)/shard_map/ppermute | solution.py:445
  56.7 10.6 %collective-permute-start.22 = (bf16[128,1024]{1,0:T(8,128)(2,1)S(1)}, bf16[128,1024]{1,0:T(8,128)(2,1)S(1)}, u32[]{:S(2)}, u32[]{:S(2)}) collective-permute-start(bf16[128,1024]{1,0:T(8,128)(2,1)S(1)} %collective-permute-done.19.refs_11_), channel_id=1, source_target_pairs={{0,1},{1,0},{2,3},{3,2},{4,5},{5,4},{6,7},{7,6},{8,9},{9,8},{10,11... | collective-permute-start | bytes 786440 | tf_op jit(solution)/shard_map/ppermute | solution.py:445
  56.7 10.6 %collective-permute-start.21 = (bf16[128,1024]{1,0:T(8,128)(2,1)S(1)}, bf16[128,1024]{1,0:T(8,128)(2,1)S(1)}, u32[]{:S(2)}, u32[]{:S(2)}) collective-permute-start(bf16[128,1024]{1,0:T(8,128)(2,1)S(1)} %collective-permute-done.18.refs_10_), channel_id=1, source_target_pairs={{0,1},{1,0},{2,3},{3,2},{4,5},{5,4},{6,7},{7,6},{8,9},{9,8},{10,11... | collective-permute-start | bytes 786440 | tf_op jit(solution)/shard_map/ppermute | solution.py:445
  63.4 5.7 %collective-permute-start.20 = (bf16[128,1024]{1,0:T(8,128)(2,1)S(1)}, bf16[128,1024]{1,0:T(8,128)(2,1)S(1)}, u32[]{:S(2)}, u32[]{:S(2)}) collective-permute-start(bf16[128,1024]{1,0:T(8,128)(2,1)S(1)} %collective-permute-done.17.refs_9_), channel_id=1, source_target_pairs={{0,1},{1,0},{2,3},{3,2},{4,5},{5,4},{6,7},{7,6},{8,9},{9,8},{10,11... | collective-permute-start | bytes 786440 | tf_op jit(solution)/shard_map/ppermute | solution.py:445
  67.3 10.2 %collective-permute-start.29 = (bf16[128,1024]{1,0:T(8,128)(2,1)S(1)}, bf16[128,1024]{1,0:T(8,128)(2,1)S(1)}, u32[]{:S(2)}, u32[]{:S(2)}) collective-permute-start(bf16[128,1024]{1,0:T(8,128)(2,1)S(1)} %copy-done.4), channel_id=1, source_target_pairs={{0,6},{1,7},{2,4},{3,5},{4,2},{5,3},{6,0},{7,1},{8,14},{9,15},{10,... | collective-permute-start | bytes 786440 | tf_op jit(solution)/shard_map/ppermute | solution.py:445
  69.1 13.4 %collective-permute-start.28 = (bf16[128,1024]{1,0:T(8,128)(2,1)S(1)}, bf16[128,1024]{1,0:T(8,128)(2,1)S(1)}, u32[]{:S(2)}, u32[]{:S(2)}) collective-permute-start(bf16[128,1024]{1,0:T(8,128)(2,1)S(1)} %copy-done.4), channel_id=1, source_target_pairs={{0,4},{1,5},{2,6},{3,7},{4,0},{5,1},{6,2},{7,3},{8,12},{9,13},{10,... | collective-permute-start | bytes 786440 | tf_op jit(solution)/shard_map/ppermute | solution.py:445
  71.0 11.6 %collective-permute-start.14 = (bf16[1024,128]{1,0:T(8,128)(2,1)}, bf16[1024,128]{1,0:T(8,128)(2,1)}, u32[]{:S(2)}, u32[]{:S(2)}) collective-permute-start(bf16[1024,128]{1,0:T(8,128)(2,1)} %collective-permute-done.10.refs_1_), channel_id=1, source_target_pairs={{0,1},{1,0},{2,3},{3,2},{4,5},{5,4},{6,7},{7,6},{8,9},{9,8},{10,11... | collective-permute-start | bytes 786440 | tf_op jit(solution)/shard_map/ppermute | solution.py:445
  71.0 23.1 %collective-permute-start.30 = (bf16[128,1024]{1,0:T(8,128)(2,1)S(1)}, bf16[128,1024]{1,0:T(8,128)(2,1)S(1)}, u32[]{:S(2)}, u32[]{:S(2)}) collective-permute-start(bf16[128,1024]{1,0:T(8,128)(2,1)S(1)} %copy-done.4), channel_id=1, source_target_pairs={{0,1},{1,0},{2,3},{3,2},{4,5},{5,4},{6,7},{7,6},{8,9},{9,8},{10,11... | collective-permute-start | bytes 786440 | tf_op jit(solution)/shard_map/ppermute | solution.py:445
  71.5 20.6 %collective-permute-start.27 = (bf16[128,1024]{1,0:T(8,128)(2,1)S(1)}, bf16[128,1024]{1,0:T(8,128)(2,1)S(1)}, u32[]{:S(2)}, u32[]{:S(2)}) collective-permute-start(bf16[128,1024]{1,0:T(8,128)(2,1)S(1)} %copy-done.4), channel_id=1, source_target_pairs={{0,2},{1,3},{2,0},{3,1},{4,6},{5,7},{6,4},{7,5},{8,10},{9,11},{10,... | collective-permute-start | bytes 786440 | tf_op jit(solution)/shard_map/ppermute | solution.py:445
  77.5 16.6 %collective-permute-start.33 = (bf16[128,1024]{1,0:T(8,128)(2,1)S(1)}, bf16[128,1024]{1,0:T(8,128)(2,1)S(1)}, u32[]{:S(2)}, u32[]{:S(2)}) collective-permute-start(bf16[128,1024]{1,0:T(8,128)(2,1)S(1)} %collective-permute-done.29.refs_3_), channel_id=1, source_target_pairs={{0,1},{1,0},{2,3},{3,2},{4,5},{5,4},{6,7},{7,6},{8,9},{9,8},{10,11... | collective-permute-start | bytes 786440 | tf_op jit(solution)/shard_map/ppermute | solution.py:445
  82.6 11.6 %collective-permute-start.32 = (bf16[128,1024]{1,0:T(8,128)(2,1)S(1)}, bf16[128,1024]{1,0:T(8,128)(2,1)S(1)}, u32[]{:S(2)}, u32[]{:S(2)}) collective-permute-start(bf16[128,1024]{1,0:T(8,128)(2,1)S(1)} %collective-permute-done.28.refs_2_), channel_id=1, source_target_pairs={{0,1},{1,0},{2,3},{3,2},{4,5},{5,4},{6,7},{7,6},{8,9},{9,8},{10,11... | collective-permute-start | bytes 786440 | tf_op jit(solution)/shard_map/ppermute | solution.py:445
  113.4 9.2 %collective-permute-start.35 = (bf16[128,1024]{1,0:T(8,128)(2,1)S(1)}, bf16[128,1024]{1,0:T(8,128)(2,1)S(1)}, u32[]{:S(2)}, u32[]{:S(2)}) collective-permute-start(bf16[128,1024]{1,0:T(8,128)(2,1)S(1)} %get-tuple-element.108), channel_id=1, source_target_pairs={{0,2},{1,3},{2,0},{3,1},{4,6},{5,7},{6,4},{7,5},{8,10},{9,11},{10,... | collective-permute-start | bytes 786440 | tf_op jit(solution)/shard_map/ppermute | solution.py:445
  114.7 13.8 %collective-permute-start.37 = (bf16[128,1024]{1,0:T(8,128)(2,1)S(1)}, bf16[128,1024]{1,0:T(8,128)(2,1)S(1)}, u32[]{:S(2)}, u32[]{:S(2)}) collective-permute-start(bf16[128,1024]{1,0:T(8,128)(2,1)S(1)} %get-tuple-element.109), channel_id=1, source_target_pairs={{0,6},{1,7},{2,4},{3,5},{4,2},{5,3},{6,0},{7,1},{8,14},{9,15},{10,... | collective-permute-start | bytes 786440 | tf_op jit(solution)/shard_map/ppermute | solution.py:445
  116.2 13.6 %collective-permute-start.36 = (bf16[128,1024]{1,0:T(8,128)(2,1)S(1)}, bf16[128,1024]{1,0:T(8,128)(2,1)S(1)}, u32[]{:S(2)}, u32[]{:S(2)}) collective-permute-start(bf16[128,1024]{1,0:T(8,128)(2,1)S(1)} %get-tuple-element.110), channel_id=1, source_target_pairs={{0,4},{1,5},{2,6},{3,7},{4,0},{5,1},{6,2},{7,3},{8,12},{9,13},{10,... | collective-permute-start | bytes 786440 | tf_op jit(solution)/shard_map/ppermute | solution.py:445
  118.0 27.7 %collective-permute-start.23 = (bf16[512,1024]{1,0:T(8,128)(2,1)S(1)}, bf16[512,1024]{1,0:T(8,128)(2,1)S(1)}, u32[]{:S(2)}, u32[]{:S(2)}) collective-permute-start(bf16[512,1024]{1,0:T(8,128)(2,1)S(1)} %convolution_convert_fusion.4), channel_id=1, source_target_pairs={{0,1},{1,0},{2,3},{3,2},{4,5},{5,4},{6,7},{7,6},{8,9},{9,8},{10,11... | collective-permute-start | bytes 3145736 | tf_op jit(solution)/shard_map/ppermute | solution.py:445
  131.4 10.2 %collective-permute-start.40 = (bf16[128,1024]{1,0:T(8,128)(2,1)S(1)}, bf16[128,1024]{1,0:T(8,128)(2,1)S(1)}, u32[]{:S(2)}, u32[]{:S(2)}) collective-permute-start(bf16[128,1024]{1,0:T(8,128)(2,1)S(1)} %fusion.63.refs_0_), channel_id=1, source_target_pairs={{0,6},{1,7},{2,4},{3,5},{4,2},{5,3},{6,0},{7,1},{8,14},{9,15},{10,... | collective-permute-start | bytes 786440 | tf_op jit(solution)/shard_map/ppermute | solution.py:445
  132.8 12.4 %collective-permute-start.39 = (bf16[128,1024]{1,0:T(8,128)(2,1)S(1)}, bf16[128,1024]{1,0:T(8,128)(2,1)S(1)}, u32[]{:S(2)}, u32[]{:S(2)}) collective-permute-start(bf16[128,1024]{1,0:T(8,128)(2,1)S(1)} %fusion.63.refs_0_), channel_id=1, source_target_pairs={{0,4},{1,5},{2,6},{3,7},{4,0},{5,1},{6,2},{7,3},{8,12},{9,13},{10,... | collective-permute-start | bytes 786440 | tf_op jit(solution)/shard_map/ppermute | solution.py:445
  133.9 11.4 %collective-permute-start.38 = (bf16[128,1024]{1,0:T(8,128)(2,1)S(1)}, bf16[128,1024]{1,0:T(8,128)(2,1)S(1)}, u32[]{:S(2)}, u32[]{:S(2)}) collective-permute-start(bf16[128,1024]{1,0:T(8,128)(2,1)S(1)} %fusion.63.refs_0_), channel_id=1, source_target_pairs={{0,2},{1,3},{2,0},{3,1},{4,6},{5,7},{6,4},{7,5},{8,10},{9,11},{10,... | collective-permute-start | bytes 786440 | tf_op jit(solution)/shard_map/ppermute | solution.py:445
  136.1 11.9 %collective-permute-start.41 = (bf16[128,1024]{1,0:T(8,128)(2,1)S(1)}, bf16[128,1024]{1,0:T(8,128)(2,1)S(1)}, u32[]{:S(2)}, u32[]{:S(2)}) collective-permute-start(bf16[128,1024]{1,0:T(8,128)(2,1)S(1)} %fusion.63.refs_0_), channel_id=1, source_target_pairs={{0,1},{1,0},{2,3},{3,2},{4,5},{5,4},{6,7},{7,6},{8,9},{9,8},{10,11... | collective-permute-start | bytes 786440 | tf_op jit(solution)/shard_map/ppermute | solution.py:445
  141.6 7.6 %collective-permute-start.44 = (bf16[128,1024]{1,0:T(8,128)(2,1)S(1)}, bf16[128,1024]{1,0:T(8,128)(2,1)S(1)}, u32[]{:S(2)}, u32[]{:S(2)}) collective-permute-start(bf16[128,1024]{1,0:T(8,128)(2,1)S(1)} %collective-permute-done.40.refs_3_), channel_id=1, source_target_pairs={{0,1},{1,0},{2,3},{3,2},{4,5},{5,4},{6,7},{7,6},{8,9},{9,8},{10,11... | collective-permute-start | bytes 786440 | tf_op jit(solution)/shard_map/ppermute | solution.py:445
  147.0 55.2 %collective-permute-start.24 = (bf16[128,1024]{1,0:T(8,128)(2,1)}, bf16[128,1024]{1,0:T(8,128)(2,1)}, u32[]{:S(2)}, u32[]{:S(2)}) collective-permute-start(bf16[128,1024]{1,0:T(8,128)(2,1)} %get-tuple-element.111), channel_id=1, source_target_pairs={{0,2},{1,3},{2,0},{3,1},{4,6},{5,7},{6,4},{7,5},{8,10},{9,11},{10,... | collective-permute-start | bytes 786440 | tf_op jit(solution)/shard_map/ppermute | solution.py:445
  148.0 54.1 %collective-permute-start.26 = (bf16[128,1024]{1,0:T(8,128)(2,1)}, bf16[128,1024]{1,0:T(8,128)(2,1)}, u32[]{:S(2)}, u32[]{:S(2)}) collective-permute-start(bf16[128,1024]{1,0:T(8,128)(2,1)} %get-tuple-element.112), channel_id=1, source_target_pairs={{0,6},{1,7},{2,4},{3,5},{4,2},{5,3},{6,0},{7,1},{8,14},{9,15},{10,... | collective-permute-start | bytes 786440 | tf_op jit(solution)/shard_map/ppermute | solution.py:445
  168.2 14.8 %collective-permute-start.45 = (bf16[512,1024]{1,0:T(8,128)(2,1)S(1)}, bf16[512,1024]{1,0:T(8,128)(2,1)S(1)}, u32[]{:S(2)}, u32[]{:S(2)}) collective-permute-start(bf16[512,1024]{1,0:T(8,128)(2,1)S(1)} %convolution_convert_fusion.3), channel_id=1, source_target_pairs={{0,1},{1,0},{2,3},{3,2},{4,5},{5,4},{6,7},{7,6},{8,9},{9,8},{10,11... | collective-permute-start | bytes 3145736 | tf_op jit(solution)/shard_map/ppermute | solution.py:445
  183.3 9.2 %collective-permute-start.46 = (bf16[128,1024]{1,0:T(8,128)(2,1)S(1)}, bf16[128,1024]{1,0:T(8,128)(2,1)S(1)}, u32[]{:S(2)}, u32[]{:S(2)}) collective-permute-start(bf16[128,1024]{1,0:T(8,128)(2,1)S(1)} %get-tuple-element.105), channel_id=1, source_target_pairs={{0,2},{1,3},{2,0},{3,1},{4,6},{5,7},{6,4},{7,5},{8,10},{9,11},{10,... | collective-permute-start | bytes 786440 | tf_op jit(solution)/shard_map/ppermute | solution.py:445
  184.6 13.5 %collective-permute-start.48 = (bf16[128,1024]{1,0:T(8,128)(2,1)S(1)}, bf16[128,1024]{1,0:T(8,128)(2,1)S(1)}, u32[]{:S(2)}, u32[]{:S(2)}) collective-permute-start(bf16[128,1024]{1,0:T(8,128)(2,1)S(1)} %get-tuple-element.106), channel_id=1, source_target_pairs={{0,6},{1,7},{2,4},{3,5},{4,2},{5,3},{6,0},{7,1},{8,14},{9,15},{10,... | collective-permute-start | bytes 786440 | tf_op jit(solution)/shard_map/ppermute | solution.py:445
  186.1 14.8 %collective-permute-start.47 = (bf16[128,1024]{1,0:T(8,128)(2,1)S(1)}, bf16[128,1024]{1,0:T(8,128)(2,1)S(1)}, u32[]{:S(2)}, u32[]{:S(2)}) collective-permute-start(bf16[128,1024]{1,0:T(8,128)(2,1)S(1)} %get-tuple-element.107), channel_id=1, source_target_pairs={{0,4},{1,5},{2,6},{3,7},{4,0},{5,1},{6,2},{7,3},{8,12},{9,13},{10,... | collective-permute-start | bytes 786440 | tf_op jit(solution)/shard_map/ppermute | solution.py:445
  192.5 12.7 %collective-permute-start.25 = (bf16[128,1024]{1,0:T(8,128)(2,1)}, bf16[128,1024]{1,0:T(8,128)(2,1)}, u32[]{:S(2)}, u32[]{:S(2)}) collective-permute-start(bf16[128,1024]{1,0:T(8,128)(2,1)} %get-tuple-element.113), channel_id=1, source_target_pairs={{0,4},{1,5},{2,6},{3,7},{4,0},{5,1},{6,2},{7,3},{8,12},{9,13},{10,... | collective-permute-start | bytes 786440 | tf_op jit(solution)/shard_map/ppermute | solution.py:445
  198.1 40.7 %collective-permute-start.61 = (bf16[64,3072]{1,0:T(8,128)(2,1)}, bf16[64,3072]{1,0:T(8,128)(2,1)}, u32[]{:S(2)}, u32[]{:S(2)}) collective-permute-start(bf16[64,3072]{1,0:T(8,128)(2,1)} %get-tuple-element.114), channel_id=1, source_target_pairs={{0,8},{8,0},{16,24},{24,16},{1,9},{9,1},{17,25},{25,17},{2,10},{10... | collective-permute-start | bytes 1179656 | tf_op jit(solution)/shard_map/ppermute | solution.py:449
  202.0 36.8 %collective-permute-start.49 = (f32[1,2176]{1,0:T(1,128)S(1)}, f32[1,2176]{1,0:T(1,128)S(1)}, u32[]{:S(2)}, u32[]{:S(2)}) collective-permute-start(f32[1,2176]{1,0:T(1,128)S(1)} %broadcast_in_dim.62), channel_id=1, source_target_pairs={{0,1},{1,0},{2,3},{3,2},{4,5},{5,4},{6,7},{7,6},{8,9},{9,8},{10,11... | collective-permute-start | bytes 26120 | tf_op jit(solution)/shard_map/ppermute | solution.py:445
  252.6 9.6 %collective-permute-start.62 = (bf16[32,3072]{1,0:T(8,128)(2,1)S(1)}, bf16[32,3072]{1,0:T(8,128)(2,1)S(1)}, u32[]{:S(2)}, u32[]{:S(2)}) collective-permute-start(bf16[32,3072]{1,0:T(8,128)(2,1)S(1)} %get-tuple-element.118), channel_id=1, source_target_pairs={{0,16},{8,24},{16,0},{24,8},{1,17},{9,25},{17,1},{25,9},{2,18},{10... | collective-permute-start | bytes 589832 | tf_op jit(solution)/shard_map/ppermute | solution.py:449
  262.2 10.2 %collective-permute-start.63 = (bf16[32,3072]{1,0:T(8,128)(2,1)S(1)}, bf16[32,3072]{1,0:T(8,128)(2,1)S(1)}, u32[]{:S(2)}, u32[]{:S(2)}) collective-permute-start(bf16[32,3072]{1,0:T(8,128)(2,1)S(1)} %add_convert_fusion.2), channel_id=1, source_target_pairs={{0,16},{8,24},{16,0},{24,8},{1,17},{9,25},{17,1},{25,9},{2,18},{10... | collective-permute-start | bytes 589832 | tf_op jit(solution)/shard_map/ppermute | solution.py:449
  272.5 11.1 %collective-permute-start.64 = (bf16[64,3072]{1,0:T(8,128)(2,1)S(1)}, bf16[64,3072]{1,0:T(8,128)(2,1)S(1)}, u32[]{:S(2)}, u32[]{:S(2)}) collective-permute-start(bf16[64,3072]{1,0:T(8,128)(2,1)S(1)} %maximum_select_fusion.1), channel_id=1, source_target_pairs={{0,8},{8,0},{16,24},{24,16},{1,9},{9,1},{17,25},{25,17},{2,10},{10... | collective-permute-start | bytes 1179656 | tf_op jit(solution)/shard_map/ppermute | solution.py:449
  (75 other events, 900.3 us)
Sparse Core Ops, SparseCore 0:
  108.4 141.3 all-reduce.1
